TPU v7x, 512 devices: a whole 4x4x16 slice. The times are simulated.
512 devices in a mesh: tensor: 16 (over y, x_hi, core), expert: 32 (over z, x_lo).
Axes of the slice: x: 4 (x_hi: 2, x_lo: 2; x = x_hi * 2 + x_lo), y: 4, z: 16, core: 2. Of those that a mesh axis runs over, the one named last changes fastest.
Arguments:
- tokens_in: bfloat16 [2048, 4096], P('expert', 'tensor'), may hold values from -6 to 6
- residual: bfloat16 [2048, 4096], P('expert', 'tensor'), may hold values from -3 to 3
- w_gate: bfloat16 [32, 4096, 1536], P('expert', 'tensor'), may hold values from -0.09375 to 0.09375
- w_up: bfloat16 [32, 4096, 1536], P('expert', 'tensor'), may hold values from -0.09375 to 0.09375
- w_down: bfloat16 [32, 1536, 4096], P('expert', None, 'tensor'), may hold values from -0.15625 to 0.15625
- expert_ids: int32 [2048, 8], P('expert'), may hold values from 0 to 31, as said below
- slot_pos: int32 [2048, 8], P('expert'), may hold values from 0 to 63, as said below
- route_weights: float32 [2048, 8], P('expert'), may hold values from 0.05 to 0.35
Outputs:
- layer_out: bfloat16 [2048, 4096], P('expert', 'tensor')
Inputs may be any that keep to these rules, and one draw needn't show every extreme that they name: `expert_ids`: each row names 8 different experts. `slot_pos`: within each aligned block of 64 rows, the choices that name one expert carry the slots 0, 1, 2 and so on, each once.
All inputs are finite; a program needn't handle non-finite values.
Results may differ from a plain program's by a relative error of at most 0.008.
Values may be sent and summed in bfloat16 or wider, within the bound.
No kernel may reach another device: no remote copies, remote signals or barrier semaphores. Data moves between devices by JAX's collectives and lax.ppermute only.
A program may use at most 64 MiB of HBM per device.

v0:
```python
import jax
import jax.numpy as jnp
from jax import lax
from jax.sharding import PartitionSpec as P


def shards(tokens_in, residual, w_gate, w_up, w_down, expert_ids, slot_pos, route_weights):
    local_rows, columns = tokens_in.shape
    choices_per = expert_ids.shape[1]
    experts = lax.axis_size("expert")
    capacity = local_rows * choices_per * 5 // (4 * experts)
    token_index = jnp.broadcast_to(
        jnp.arange(local_rows, dtype=jnp.int32)[:, None], expert_ids.shape
    )
    keep = slot_pos < capacity
    dummy = experts * capacity
    flat = jnp.where(keep, expert_ids * capacity + slot_pos, dummy)
    table = (
        jnp.full((dummy + 1,), local_rows, jnp.int32)
        .at[flat.reshape(-1)]
        .set(token_index.reshape(-1))
    )
    padded = jnp.concatenate([tokens_in, jnp.zeros((1, columns), jnp.bfloat16)], axis=0)
    outgoing = padded[table[:-1]].reshape(experts, capacity, columns)
    arrived = lax.all_to_all(outgoing, "expert", split_axis=0, concat_axis=0, tiled=True)
    buffer_rows = arrived.reshape(experts * capacity, columns)
    gate_matrix = w_gate[0]
    up_weight_matrix = w_up[0]
    down_mat = w_down[0]
    gate_part = jnp.dot(buffer_rows, gate_matrix, preferred_element_type=jnp.float32)
    up_part = jnp.dot(buffer_rows, up_weight_matrix, preferred_element_type=jnp.float32)
    gate_sum, up_sum = lax.psum((gate_part, up_part), "tensor")
    hidden = (jax.nn.silu(gate_sum) * up_sum).astype(jnp.bfloat16)
    expert_out = jnp.dot(hidden, down_mat, preferred_element_type=jnp.float32).astype(jnp.bfloat16)
    returned = lax.all_to_all(
        expert_out.reshape(experts, capacity, columns),
        "expert",
        split_axis=0,
        concat_axis=0,
        tiled=True,
    )
    returned_flat = jnp.concatenate(
        [returned.reshape(experts * capacity, columns), jnp.zeros((1, columns), jnp.bfloat16)],
        axis=0,
    )
    picked = returned_flat[flat].astype(jnp.float32)
    mixed = residual.astype(jnp.float32) + jnp.einsum("nk,nkd->nd", route_weights, picked)
    return mixed.astype(jnp.bfloat16)


def solution(mesh):
    in_specs = (
        P("expert", "tensor"),
        P("expert", "tensor"),
        P("expert", "tensor", None),
        P("expert", "tensor", None),
        P("expert", None, "tensor"),
        P("expert", None),
        P("expert", None),
        P("expert", None),
    )
    out_specs = P("expert", "tensor")
    return jax.shard_map(shards, mesh=mesh, in_specs=in_specs, out_specs=out_specs, check_vma=False)
```

profile of v0, /device:TPU:1, one launch (start us, length us, event | category | flops | bytes accessed | tf_op | source)
XLA Modules:
  0.0 309.5 jit_solution(16337493639403184929)
XLA Ops:
  6.5 0.0 copy-start
  6.5 0.0 all-reduce.5.cloned.1.call-start
  6.5 0.8 compare_select_fusion.1
  7.3 0.1 copy.9
  7.4 0.1 reshape.46
  7.5 0.1 reshape.72
  7.6 2.4 scatter_custom_fusion
  10.1 0.8 concatenate.6
  10.9 2.8 gather_fusion
  13.6 0.0 copy-start.1
  13.6 0.1 reshape.48
  13.7 42.6 %all_to_all.10 = bf16[32,20,256]{2,1,0:T(8,128)(2,1)S(1)} all-to-all(bf16[32,20,256]{2,1,0:T(8,128)(2,1)S(1)} %reshape.48), channel_id=1, replica_groups=mesh['tensor'=16,'expert'=32] {'expert'}, dimensions={0} | all-to-all | bytes 655360 | tf_op jit(solution)/shard_map/all_to_all | solution.py:25
  56.3 0.1 reshape.49
  56.4 0.0 copy-done
  56.4 2.6 fusion.3
  59.0 0.0 copy-done.1
  59.0 2.6 fusion.5
  61.6 0.0 copy-start.4
  61.6 0.0 all-reduce.5.cloned.1.call-update
  61.6 196.6 %all-reduce.5.cloned.1.call-done = (f32[640,1536]{1,0:T(8,128)}, f32[640,1536]{1,0:T(8,128)}) async-done(((f32[640,1536]{1,0:T(8,128)}, f32[640,1536]{1,0:T(8,128)}), (f32[640,1536]{1,0:T(8,128)}, f32[640,1536]{1,0:T(8,128)})) %all-reduce.5.cloned.1.call-update) | async-done | bytes 7864336 | tf_op jit(solution)/shard_map/psum | solution.py:32
  258.2 0.0 copy-done.4
  258.2 0.0 copy-start.3
  258.2 4.5 %fusion.1 = bf16[640,256]{1,0:T(8,128)(2,1)S(1)} fusion(f32[640,1536]{1,0:T(8,128)} %get-tuple-element.5, f32[640,1536]{1,0:T(8,128)} %get-tuple-element.6, bf16[1,1536,256]{2,1,0:T(8,128)(2,1)S(1)} %copy-done.4), kind=kOutput, calls=%fused_computation.5 | convolution fusion | flops 509378560 | bytes 8978432 | tf_op jit(solution)/shard_map/dot_general | solution.py:34
  262.8 0.0 copy-start.2
  262.8 0.8 reshape.50
  263.6 12.3 %all-to-all-start.1 = ((bf16[32,20,256]{2,1,0:T(8,128)(2,1)}), bf16[32,20,256]{2,1,0:T(8,128)(2,1)S(1)}, u32[]{:S(2)}, u32[]{:S(2)}) async-start(bf16[32,20,256]{2,1,0:T(8,128)(2,1)} %reshape.50), calls=%async_computation.1 | async-start | bytes 786432 | tf_op jit(solution)/shard_map/all_to_all | solution.py:35
  275.9 0.1 copy.10
  276.0 0.1 reshape.62
  276.1 0.0 copy-done.3
  276.1 0.1 copy.11
  276.2 23.5 %all-to-all-done.1 = bf16[32,20,256]{2,1,0:T(8,128)(2,1)S(1)} async-done(((bf16[32,20,256]{2,1,0:T(8,128)(2,1)}), bf16[32,20,256]{2,1,0:T(8,128)(2,1)S(1)}, u32[]{:S(2)}, u32[]{:S(2)}) %all-to-all-start.1) | async-done | bytes 327712 | tf_op jit(solution)/shard_map/all_to_all | solution.py:35
  299.7 0.1 reshape.51
  299.8 2.0 gather_fusion.1
  301.8 0.2 fusion.7
  302.0 0.0 copy-done.2
  302.0 0.6 fusion.9
  (6 shorter events, 0.1 us)
Async XLA Ops:
  6.5 49.8 %copy-start = (bf16[1,256,1536]{2,1,0:T(8,128)(2,1)S(1)}, bf16[1,256,1536]{2,1,0:T(8,128)(2,1)}, u32[]{:S(2)}) copy-start(bf16[1,256,1536]{2,1,0:T(8,128)(2,1)} %param.11) | copy-start | bytes 2359300
  6.5 251.7 %all-reduce.5.cloned.1.call-start = ((), (), s32[]{:S(2)}) async-start(), calls=%async_computation.2 | async-start | bytes 15728640 | tf_op jit(solution)/shard_map/psum | solution.py:32
  13.6 45.4 %copy-start.1 = (bf16[1,256,1536]{2,1,0:T(8,128)(2,1)S(1)}, bf16[1,256,1536]{2,1,0:T(8,128)(2,1)}, u32[]{:S(2)}) copy-start(bf16[1,256,1536]{2,1,0:T(8,128)(2,1)} %param.10) | copy-start | bytes 2359300
  61.6 196.6 %copy-start.4 = (bf16[1,1536,256]{2,1,0:T(8,128)(2,1)S(1)}, bf16[1,1536,256]{2,1,0:T(8,128)(2,1)}, u32[]{:S(2)}) copy-start(bf16[1,1536,256]{2,1,0:T(8,128)(2,1)} %param.12) | copy-start | bytes 2359300
  258.2 17.8 %copy-start.3 = (f32[64,8]{0,1:T(8,128)S(1)}, f32[64,8]{0,1:T(8,128)}, u32[]{:S(2)}) copy-start(f32[64,8]{0,1:T(8,128)} %param.15) | copy-start | bytes 6148
  262.8 39.2 %copy-start.2 = (bf16[64,256]{1,0:T(8,128)(2,1)S(1)}, bf16[64,256]{1,0:T(8,128)(2,1)}, u32[]{:S(2)}) copy-start(bf16[64,256]{1,0:T(8,128)(2,1)} %param.9) | copy-start | bytes 98308
  263.6 36.1 %all-to-all-start.1 = ((bf16[32,20,256]{2,1,0:T(8,128)(2,1)}), bf16[32,20,256]{2,1,0:T(8,128)(2,1)S(1)}, u32[]{:S(2)}, u32[]{:S(2)}) async-start(bf16[32,20,256]{2,1,0:T(8,128)(2,1)} %reshape.50), calls=%async_computation.1 | async-start | bytes 786432 | tf_op jit(solution)/shard_map/all_to_all | solution.py:35
Sparse Core Ops, SparseCore 0:
  61.8 196.4 all-reduce.4
where the time goes:
time: 313 us; the launch traced here: 309 us
  waiting for transfers between devices  220 us (70%)
  blocking collectives  42.6 us (14%)
  between operations  13.5 us (4%)
  starting transfers between devices  12.3 us (4%)
  matrix products  9.98 us (3%)
  local copies, waits for them, and re-layouts  9.54 us (3%)
    psum x1, waiting for transfers between devices, shards(): gate_sum, up_sum = lax.psum((gate_part, up_part), 'tensor')  197 us
    all_to_all x1, blocking collectives, shards(): lax.all_to_all(outgoing, 'expert', split_axis=0, concat_axis=0, tiled=True)  42.6 us
    all_to_all x1, waiting for transfers between devices, shards(): lax.all_to_all(expert_out.reshape(experts, capacity, columns), 'expert',...  23.5 us
    all_to_all x1, starting transfers between devices, shards(): lax.all_to_all(expert_out.reshape(experts, capacity, columns), 'expert',...  12.3 us
  transfers between devices with their start and end apart: 2, of which 2 were waited for; matrix products, arithmetic and copies ran while one was open for 0% of the time, Pallas kernels for 0%

commit v1 on v0

v1 whole, which is shorter than its diff:
```python
import functools

import jax
import jax.numpy as jnp
from jax import lax
from jax.experimental import pallas as pl
from jax.experimental.pallas import tpu as pltpu
from jax.sharding import Mesh, PartitionSpec as P

BF = jnp.bfloat16
F32 = jnp.float32
T = ("y", "xh", "c")
R = ("y", "xh")
E = ("z", "xl")
VMEM = pl.BlockSpec(memory_space=pltpu.VMEM)


def call(body, out, *args, name, limit=48 << 20, scratch=(), flops=0, moved=0):
    return pl.pallas_call(
        body,
        out_shape=out,
        in_specs=[VMEM] * len(args),
        out_specs=jax.tree.map(lambda _: VMEM, out),
        scratch_shapes=list(scratch),
        compiler_params=pltpu.CompilerParams(vmem_limit_bytes=limit),
        cost_estimate=pl.CostEstimate(flops=flops, bytes_accessed=moved, transcendentals=0),
        name=name,
    )(*args)


def row_codes(rows):
    r = lax.broadcasted_iota(jnp.int32, (rows, 1), 0)
    base = (r // 8) * 64
    j = lax.rem(r, 8)
    return base + j, base + 8 + j, base + 16 + lax.rem(j, 4), j < 4


def dispatch_body(x_ref, ids_ref, slot_ref, out_ref):
    code = ids_ref[...] * 64 + slot_ref[...]
    x = x_ref[...]
    c0, c1, c2, low = row_codes(out_ref.shape[0])

    def pick(c):
        hit = c == code[0:1, :]
        for k in range(1, code.shape[0]):
            hit = hit | (c == code[k : k + 1, :])
        return jnp.dot(
            jnp.where(hit, 1.0, 0.0).astype(BF), x, preferred_element_type=F32
        )

    out_ref[:, 0:256] = pick(c0).astype(BF)
    out_ref[:, 256:512] = pick(c1).astype(BF)
    tail = pick(c2)
    out_ref[:, 512:640] = jnp.where(low, tail[:, 0:128], tail[:, 128:256]).astype(BF)


def rows_of(a_ref, x_ref):
    n = a_ref.shape[0]
    x_ref[0:n, :] = a_ref[:, 0:256]
    x_ref[n : 2 * n, :] = a_ref[:, 256:512]
    t = a_ref[:, 512:640].astype(F32).reshape(n // 16, 2, 8, 128)
    t0, t1 = t[:, 0], t[:, 1]
    low = lax.broadcasted_iota(jnp.int32, t0.shape, 1) < 4
    b0 = jnp.where(low, t0, pltpu.roll(t1, 4, 1))
    b1 = jnp.where(low, pltpu.roll(t0, 4, 1), t1)
    x_ref[2 * n :, 0:128] = b0.reshape(n // 2, 128).astype(BF)
    x_ref[2 * n :, 128:256] = b1.reshape(n // 2, 128).astype(BF)


def up_body(a_ref, b_ref, wga_ref, wgb_ref, wua_ref, wub_ref, out_ref, xa, xb):
    rows_of(a_ref, xa)
    rows_of(b_ref, xb)
    half = wga_ref.shape[1]

    @pl.loop(0, out_ref.shape[0] // 128)
    def _(i):
        s = pl.ds(pl.multiple_of(i * 128, 128), 128)
        a, b = xa[s, :], xb[s, :]
        for w, v, o in ((wga_ref, wgb_ref, 0), (wua_ref, wub_ref, half)):
            out_ref[s, o : o + half] = (
                jnp.dot(a, w[...], preferred_element_type=F32)
                + jnp.dot(b, v[...], preferred_element_type=F32)
            ).astype(BF)


def act_body(p_ref, h_ref):
    rows = p_ref.shape[0] // 8
    half = h_ref.shape[1]

    @pl.loop(0, rows // 8)
    def _(i):
        def total(o):
            t = None
            for d in range(8):
                v = p_ref[pl.ds(pl.multiple_of(d * rows + i * 8, 8), 8), o : o + half]
                t = v.astype(F32) if t is None else t + v.astype(F32)
            return t

        g, u = total(0), total(half)
        h = (g / (1.0 + jnp.exp(-g)) * u).astype(BF)
        for d in range(8):
            h_ref[pl.ds(pl.multiple_of(d * rows + i * 8, 8), 8), :] = h


def down_body(ha_ref, hb_ref, wa_ref, wb_ref, out_ref):
    n = out_ref.shape[0]

    def rows(s, m):
        return jnp.dot(ha_ref[s : s + m, :], wa_ref[...], preferred_element_type=F32) + jnp.dot(
            hb_ref[s : s + m, :], wb_ref[...], preferred_element_type=F32
        )

    out_ref[:, 0:256] = rows(0, n).astype(BF)
    out_ref[:, 256:512] = rows(n, n).astype(BF)
    t = rows(2 * n, n // 2)
    b0 = t[:, 0:128].reshape(n // 16, 8, 128)
    b1 = t[:, 128:256].reshape(n // 16, 8, 128)
    low = lax.broadcasted_iota(jnp.int32, b0.shape, 1) < 4
    t0 = jnp.where(low, b0, pltpu.roll(b1, 4, 1))
    t1 = jnp.where(low, pltpu.roll(b0, 4, 1), b1)
    out_ref[:, 512:640] = jnp.stack([t0, t1], axis=1).reshape(n, 128).astype(BF)


def combine_body(r_ref, res_ref, ids_ref, slot_ref, w_ref, out_ref):
    code = ids_ref[...] * 64 + slot_ref[...]
    w = w_ref[...]
    c0, c1, c2, low = row_codes(r_ref.shape[0])

    def weights(c):
        t = jnp.where(c == code[0:1, :], w[0:1, :], 0.0)
        for k in range(1, code.shape[0]):
            t = t + jnp.where(c == code[k : k + 1, :], w[k : k + 1, :], 0.0)
        return t

    def mix(m, v):
        hi = m.astype(BF)
        lo = (m - hi.astype(F32)).astype(BF)
        dims = (((0,), (0,)), ((), ()))
        return lax.dot_general(hi, v, dims, preferred_element_type=F32) + lax.dot_general(
            lo, v, dims, preferred_element_type=F32
        )

    total = res_ref[...].astype(F32)
    total += mix(weights(c0), r_ref[:, 0:256]) + mix(weights(c1), r_ref[:, 256:512])
    tail = weights(c2)
    v = r_ref[:, 512:640]
    out_ref[:, 0:128] = (total[:, 0:128] + mix(jnp.where(low, tail, 0.0), v)).astype(BF)
    out_ref[:, 128:256] = (total[:, 128:256] + mix(jnp.where(low, 0.0, tail), v)).astype(BF)


def swap(x):
    return lax.ppermute(x, "c", [(0, 1), (1, 0)])


def spread(x, axes):
    return lax.all_to_all(x, axes, split_axis=0, concat_axis=0, tiled=True)


def shards(tokens_in, residual, w_gate, w_up, w_down, expert_ids, slot_pos, route_weights):
    ids, slots, weights = expert_ids.T, slot_pos.T, route_weights.T
    core = lax.axis_index("c")
    half = w_gate.shape[2] // 2
    sds = jax.ShapeDtypeStruct
    experts = lax.axis_size(E)
    rows = experts * 20

    def halves(w, axis):
        mine = lax.dynamic_slice_in_dim(w, core * half, half, axis)
        other = lax.dynamic_slice_in_dim(w, (1 - core) * half, half, axis)
        return mine, other

    outgoing = call(
        dispatch_body, sds((experts * 8, 640), BF), tokens_in, ids, slots, name="dispatch"
    )
    gate_mine, gate_other = halves(w_gate[0], 1)
    up_mine, up_other = halves(w_up[0], 1)
    gate_recv, up_recv = swap(gate_other), swap(up_other)
    arrived = spread(outgoing, E)
    arrived_b = swap(arrived)
    partial = call(
        up_body,
        sds((rows, 2 * half), BF),
        arrived, arrived_b, gate_mine, gate_recv, up_mine, up_recv,
        scratch=[pltpu.VMEM((rows, 256), BF)] * 2,
        name="gate_up",
    )
    parts = spread(partial, R)
    hidden = call(act_body, sds((rows, half), BF), parts, name="act")
    hidden = spread(hidden, R)
    hidden_b = swap(hidden)
    down_mine, down_other = halves(w_down[0], 0)
    result = call(
        down_body, sds((experts * 8, 640), BF), hidden, hidden_b, down_mine, down_other,
        name="down",
    )
    returned = spread(result, E)
    return call(
        combine_body, sds(tokens_in.shape, BF), returned, residual, ids, slots, weights,
        name="combine",
    )


def solution(mesh):
    fine = Mesh(mesh.devices.reshape(4, 2, 2, 16, 2), T + E)
    in_specs = (
        P(E, T),
        P(E, T),
        P(E, T, None),
        P(E, T, None),
        P(E, None, T),
        P(E, None),
        P(E, None),
        P(E, None),
    )
    return jax.shard_map(
        shards, mesh=fine, in_specs=in_specs, out_specs=P(E, T), check_vma=False
    )
```

time: 313 us -> 138 us (0.44)
  waiting for transfers between devices: 220 us -> 20.5 us
  blocking collectives: 42.6 us -> 77 us
  starting transfers between devices: 12.3 us -> 30.6 us
  between operations: 13.5 us -> 0.17 us
  matrix products: 9.98 us -> 0 us
  local copies, waits for them, and re-layouts: 9.54 us -> 3.46 us
  Pallas kernels: 0 us -> 5.53 us
    psum x1 -> x0, waiting for transfers between devices: 197 us -> none  [shards(): gate_sum, up_sum = lax.psum((gate_part, up_part), 'tensor')]
    all_to_all x1 -> x3, blocking collectives: 42.6 us -> 77 us  [spread(): return lax.all_to_all(x, axes, split_axis=0, concat_axis=0, tiled=True)]
    ppermute x0 -> x4, starting transfers between devices: none -> 13.6 us  [swap(): return lax.ppermute(x, 'c', [(0, 1), (1, 0)])]
    dot_general x4 -> x0, matrix products: 9.98 us -> none  [the longest x1 4.51 us: shards(): jnp.dot(hidden, down_mat, preferred_element_type=jnp.float32)]
    all_to_all x1, waiting for transfers between devices: 23.5 us -> 17.2 us  [spread(): return lax.all_to_all(x, axes, split_axis=0, concat_axis=0, tiled=True)]
    pallas_call x0 -> x5, Pallas kernels: none -> 5.53 us  [call(): pl.pallas_call(body, out_shape=out, in_specs=[VMEM] * len(args), out_spec...]
    gather x2 -> x0, local copies, waits for them, and re-layouts: 4.72 us -> none  [the longest x1 2.76 us: shards(): outgoing = padded[table[:-1]].reshape(experts, capacity, columns)]
    all_to_all x1, starting transfers between devices: 12.3 us -> 17 us  [spread(): return lax.all_to_all(x, axes, split_axis=0, concat_axis=0, tiled=True)]
  transfers between devices with their start and end apart: 2 -> 5, of which waited for: 2 -> 3; matrix products, arithmetic and copies ran while one was open for 0% -> 1% of each run, Pallas kernels for 0% -> 0%
where the time goes in v1:
time: 138 us; the launch traced here: 137 us
  blocking collectives  77 us (56%)
  starting transfers between devices  30.6 us (22%)
  waiting for transfers between devices  20.5 us (15%)
  Pallas kernels  5.53 us (4%)
  local copies, waits for them, and re-layouts  3.46 us (3%)
    all_to_all x3, blocking collectives, spread(): return lax.all_to_all(x, axes, split_axis=0, concat_axis=0, tiled=True)  77 us
    all_to_all x1, waiting for transfers between devices, spread(): return lax.all_to_all(x, axes, split_axis=0, concat_axis=0, tiled=True)  17.2 us
    all_to_all x1, starting transfers between devices, spread(): return lax.all_to_all(x, axes, split_axis=0, concat_axis=0, tiled=True)  17 us
    ppermute x4, starting transfers between devices, swap(): return lax.ppermute(x, 'c', [(0, 1), (1, 0)])  13.6 us
    pallas_call x5, Pallas kernels, call(): pl.pallas_call(body, out_shape=out, in_specs=[VMEM] * len(args), out_spec...  5.53 us
    ppermute x4, waiting for transfers between devices, swap(): return lax.ppermute(x, 'c', [(0, 1), (1, 0)])  3.26 us
  transfers between devices with their start and end apart: 5, of which 3 were waited for; matrix products, arithmetic and copies ran while one was open for 1% of the time, Pallas kernels for 0%

profile of v1, /device:TPU:1, one launch (start us, length us, event | category | flops | bytes accessed | tf_op | source)
XLA Modules:
  0.0 137.2 jit_solution(8292320273834113800)
XLA Ops:
  0.0 0.0 copy-start
  0.0 0.8 copy-done
  0.8 0.0 copy-start.2
  0.8 0.7 copy-done.2
  1.4 0.0 copy-start.4
  1.4 0.7 copy-done.4
  2.1 0.0 copy-start.7
  2.1 1.2 dispatch.1
  3.3 17.0 %all-to-all-start = ((bf16[32,8,640]{2,1,0:T(8,128)(2,1)}), bf16[32,8,640]{2,1,0:T(8,128)(2,1)S(1)}, u32[]{:S(2)}, u32[]{:S(2)}) async-start(bf16[32,8,640]{2,1,0:T(8,128)(2,1)} %bitcast.2), calls=%async_computation | async-start | bytes 655360 | tf_op jit(solution)/shard_map/all_to_all | solution.py:156
  20.3 1.2 dynamic-slice_bitcast_fusion.4
  21.5 2.9 %collective-permute-start.1 = (bf16[256,768]{1,0:T(8,128)(2,1)S(1)}, bf16[256,768]{1,0:T(8,128)(2,1)S(1)}, u32[]{:S(2)}, u32[]{:S(2)}) collective-permute-start(bf16[256,768]{1,0:T(8,128)(2,1)S(1)} %get-tuple-element.9), channel_id=1, source_target_pairs={{0,32},{32,0},{1,33},{33,1},{2,34},{34,2},{3,35},{35,3},{4,36},{36... | collective-permute-start | bytes 1179656 | tf_op jit(solution)/shard_map/ppermute | solution.py:152
  24.4 0.0 copy-done.7
  24.4 0.1 dynamic-slice_bitcast_fusion.2
  24.4 1.9 %collective-permute-start.2 = (bf16[256,768]{1,0:T(8,128)(2,1)S(1)}, bf16[256,768]{1,0:T(8,128)(2,1)S(1)}, u32[]{:S(2)}, u32[]{:S(2)}) collective-permute-start(bf16[256,768]{1,0:T(8,128)(2,1)S(1)} %get-tuple-element.7), channel_id=1, source_target_pairs={{0,32},{32,0},{1,33},{33,1},{2,34},{34,2},{3,35},{35,3},{4,36},{36... | collective-permute-start | bytes 1179656 | tf_op jit(solution)/shard_map/ppermute | solution.py:152
  26.4 17.2 %all-to-all-done = bf16[32,8,640]{2,1,0:T(8,128)(2,1)S(1)} async-done(((bf16[32,8,640]{2,1,0:T(8,128)(2,1)}), bf16[32,8,640]{2,1,0:T(8,128)(2,1)S(1)}, u32[]{:S(2)}, u32[]{:S(2)}) %all-to-all-start) | async-done | bytes 327712 | tf_op jit(solution)/shard_map/all_to_all | solution.py:156
  43.6 4.3 %collective-permute-start = (bf16[256,640]{1,0:T(8,128)(2,1)S(1)}, bf16[256,640]{1,0:T(8,128)(2,1)S(1)}, u32[]{:S(2)}, u32[]{:S(2)}) collective-permute-start(bf16[256,640]{1,0:T(8,128)(2,1)S(1)} %bitcast.28), channel_id=1, source_target_pairs={{0,32},{32,0},{1,33},{33,1},{2,34},{34,2},{3,35},{35,3},{4,36},{36... | collective-permute-start | bytes 983048 | tf_op jit(solution)/shard_map/ppermute | solution.py:152
  47.8 0.0 collective-permute-done.1.wgb_ref
  47.8 0.0 collective-permute-done.2.wub_ref
  47.8 1.2 collective-permute-done.b_ref
  49.1 1.9 %gate_up.1 = bf16[640,1536]{1,0:T(8,128)(2,1)S(1)} custom-call(bf16[256,640]{1,0:T(8,128)(2,1)S(1)} %bitcast.29, bf16[256,640]{1,0:T(8,128)(2,1)S(1)} %collective-permute-done.b_ref, bf16[256,768]{1,0:T(8,128)(2,1)S(1)} %get-tuple-element.10.wga_ref, bf16[256,768]{1,0:T(8,128)(2,1)S(1)} %collective-permute-done.1.wgb_ref, ...), custom_call_target="tpu_custom_call" | custom-call | tf_op jit(solution)/shard_map/gate_up/pallas_call | solution.py:19
  51.0 32.4 %all_to_all.44 = bf16[8,80,1536]{2,1,0:T(8,128)(2,1)S(1)} all-to-all(bf16[8,80,1536]{2,1,0:T(8,128)(2,1)S(1)} %bitcast.23), channel_id=1, replica_groups=mesh['y'=4,'xh'=2,'c'=2,'z'=16,'xl'=2] {'y','xh'}, dimensions={0} | all-to-all | bytes 3932160 | tf_op jit(solution)/shard_map/all_to_all | solution.py:156
  83.4 0.0 copy-start.8
  83.4 0.4 act.1
  83.8 17.7 %all_to_all.45 = bf16[8,80,768]{2,1,0:T(8,128)(2,1)S(1)} all-to-all(bf16[8,80,768]{2,1,0:T(8,128)(2,1)S(1)} %bitcast.27), channel_id=1, replica_groups=mesh['y'=4,'xh'=2,'c'=2,'z'=16,'xl'=2] {'y','xh'}, dimensions={0} | all-to-all | bytes 1966080 | tf_op jit(solution)/shard_map/all_to_all | solution.py:156
  101.5 4.6 %collective-permute-start.3 = (bf16[640,768]{1,0:T(8,128)(2,1)S(1)}, bf16[640,768]{1,0:T(8,128)(2,1)S(1)}, u32[]{:S(2)}, u32[]{:S(2)}) collective-permute-start(bf16[640,768]{1,0:T(8,128)(2,1)S(1)} %bitcast.25), channel_id=1, source_target_pairs={{0,32},{32,0},{1,33},{33,1},{2,34},{34,2},{3,35},{35,3},{4,36},{36... | collective-permute-start | bytes 2949128 | tf_op jit(solution)/shard_map/ppermute | solution.py:152
  106.1 0.0 copy-done.8
  106.1 0.1 dynamic-slice_bitcast_fusion
  106.2 0.0 copy-start.1
  106.2 0.0 copy-start.3
  106.2 0.0 copy-start.5
  106.2 0.0 copy-start.6
  106.2 2.0 %collective-permute-done.3.hb_ref = bf16[640,768]{1,0:T(8,128)(2,1)S(1)} collective-permute-done((bf16[640,768]{1,0:T(8,128)(2,1)S(1)}, bf16[640,768]{1,0:T(8,128)(2,1)S(1)}, u32[]{:S(2)}, u32[]{:S(2)}) %collective-permute-start.3) | collective-permute-done | bytes 983072 | tf_op jit(solution)/shard_map/ppermute | solution.py:152
  108.3 0.7 down.1
  109.0 26.9 %all_to_all.46 = bf16[32,8,640]{2,1,0:T(8,128)(2,1)S(1)} all-to-all(bf16[32,8,640]{2,1,0:T(8,128)(2,1)S(1)} %bitcast.30), channel_id=1, replica_groups=mesh['y'=4,'xh'=2,'c'=2,'z'=16,'xl'=2] {'z','xl'}, dimensions={0} | all-to-all | bytes 655360 | tf_op jit(solution)/shard_map/all_to_all | solution.py:156
  135.9 0.0 copy-done.1
  135.9 0.0 copy-done.3
  135.9 0.0 copy-done.5
  135.9 0.0 copy-done.6
  135.9 1.3 combine.1
Async XLA Ops:
  0.0 0.8 copy-start
  0.8 0.7 copy-start.2
  1.4 0.7 copy-start.4
  2.1 22.2 %copy-start.7 = (bf16[1,256,1536]{2,1,0:T(8,128)(2,1)S(1)}, bf16[1,256,1536]{2,1,0:T(8,128)(2,1)}, u32[]{:S(2)}) copy-start(bf16[1,256,1536]{2,1,0:T(8,128)(2,1)} %param.11) | copy-start | bytes 2359300
  3.3 40.2 %all-to-all-start = ((bf16[32,8,640]{2,1,0:T(8,128)(2,1)}), bf16[32,8,640]{2,1,0:T(8,128)(2,1)S(1)}, u32[]{:S(2)}, u32[]{:S(2)}) async-start(bf16[32,8,640]{2,1,0:T(8,128)(2,1)} %bitcast.2), calls=%async_computation | async-start | bytes 655360 | tf_op jit(solution)/shard_map/all_to_all | solution.py:156
  21.5 26.3 %collective-permute-start.1 = (bf16[256,768]{1,0:T(8,128)(2,1)S(1)}, bf16[256,768]{1,0:T(8,128)(2,1)S(1)}, u32[]{:S(2)}, u32[]{:S(2)}) collective-permute-start(bf16[256,768]{1,0:T(8,128)(2,1)S(1)} %get-tuple-element.9), channel_id=1, source_target_pairs={{0,32},{32,0},{1,33},{33,1},{2,34},{34,2},{3,35},{35,3},{4,36},{36... | collective-permute-start | bytes 1179656 | tf_op jit(solution)/shard_map/ppermute | solution.py:152
  24.4 23.4 %collective-permute-start.2 = (bf16[256,768]{1,0:T(8,128)(2,1)S(1)}, bf16[256,768]{1,0:T(8,128)(2,1)S(1)}, u32[]{:S(2)}, u32[]{:S(2)}) collective-permute-start(bf16[256,768]{1,0:T(8,128)(2,1)S(1)} %get-tuple-element.7), channel_id=1, source_target_pairs={{0,32},{32,0},{1,33},{33,1},{2,34},{34,2},{3,35},{35,3},{4,36},{36... | collective-permute-start | bytes 1179656 | tf_op jit(solution)/shard_map/ppermute | solution.py:152
  43.6 5.5 %collective-permute-start = (bf16[256,640]{1,0:T(8,128)(2,1)S(1)}, bf16[256,640]{1,0:T(8,128)(2,1)S(1)}, u32[]{:S(2)}, u32[]{:S(2)}) collective-permute-start(bf16[256,640]{1,0:T(8,128)(2,1)S(1)} %bitcast.28), channel_id=1, source_target_pairs={{0,32},{32,0},{1,33},{33,1},{2,34},{34,2},{3,35},{35,3},{4,36},{36... | collective-permute-start | bytes 983048 | tf_op jit(solution)/shard_map/ppermute | solution.py:152
  83.4 22.7 %copy-start.8 = (bf16[1,1536,256]{2,1,0:T(8,128)(2,1)S(1)}, bf16[1,1536,256]{2,1,0:T(8,128)(2,1)}, u32[]{:S(2)}) copy-start(bf16[1,1536,256]{2,1,0:T(8,128)(2,1)} %param.12) | copy-start | bytes 2359300
  101.5 6.8 %collective-permute-start.3 = (bf16[640,768]{1,0:T(8,128)(2,1)S(1)}, bf16[640,768]{1,0:T(8,128)(2,1)S(1)}, u32[]{:S(2)}, u32[]{:S(2)}) collective-permute-start(bf16[640,768]{1,0:T(8,128)(2,1)S(1)} %bitcast.25), channel_id=1, source_target_pairs={{0,32},{32,0},{1,33},{33,1},{2,34},{34,2},{3,35},{35,3},{4,36},{36... | collective-permute-start | bytes 2949128 | tf_op jit(solution)/shard_map/ppermute | solution.py:152
  106.2 29.7 %copy-start.1 = (bf16[64,256]{1,0:T(8,128)(2,1)S(1)}, bf16[64,256]{1,0:T(8,128)(2,1)}, u32[]{:S(2)}) copy-start(bf16[64,256]{1,0:T(8,128)(2,1)} %res_ref.1) | copy-start | bytes 98308
  106.2 29.7 %copy-start.3 = (s32[64,8]{0,1:T(8,128)S(1)}, s32[64,8]{0,1:T(8,128)}, u32[]{:S(2)}) copy-start(s32[64,8]{0,1:T(8,128)} %param.13) | copy-start | bytes 6148
  106.2 29.7 %copy-start.5 = (s32[64,8]{0,1:T(8,128)S(1)}, s32[64,8]{0,1:T(8,128)}, u32[]{:S(2)}) copy-start(s32[64,8]{0,1:T(8,128)} %param.14) | copy-start | bytes 6148
  106.2 29.7 %copy-start.6 = (f32[64,8]{0,1:T(8,128)S(1)}, f32[64,8]{0,1:T(8,128)}, u32[]{:S(2)}) copy-start(f32[64,8]{0,1:T(8,128)} %param.15) | copy-start | bytes 6148

commit v2 on v1

v2 whole, which is shorter than its diff:
```python
import jax
import jax.numpy as jnp
from jax import lax
from jax.experimental import pallas as pl
from jax.experimental.pallas import tpu as pltpu
from jax.sharding import Mesh, PartitionSpec as P

BF = jnp.bfloat16
F32 = jnp.float32
T = ("y", "xh", "c")
E = ("z", "xl")
VMEM = pl.BlockSpec(memory_space=pltpu.VMEM)
HBM = pl.BlockSpec(memory_space=pltpu.HBM)


def call(body, out, *args, name, limit=48 << 20, scratch=(), flops=0, moved=0, stay=()):
    return pl.pallas_call(
        body,
        out_shape=out,
        in_specs=[HBM if i in stay else VMEM for i in range(len(args))],
        out_specs=jax.tree.map(lambda _: HBM if stay else VMEM, out),
        scratch_shapes=list(scratch),
        compiler_params=pltpu.CompilerParams(vmem_limit_bytes=None if stay else limit),
        cost_estimate=pl.CostEstimate(flops=flops, bytes_accessed=moved, transcendentals=0),
        name=name,
    )(*args)


def row_codes(rows, first):
    r = lax.broadcasted_iota(jnp.int32, (rows, 1), 0)
    base = (r // 8) * 64 + first
    j = lax.rem(r, 8)
    return base + j, base + 8 + j // 4, lax.rem(j, 4)


def columns_body(gate_hbm, up_hbm, cols_hbm, sems):
    width, half = cols_hbm.shape[0] // 2, cols_hbm.shape[1] // 2
    core = lax.axis_index("c")
    copies = []
    for k, w in enumerate((gate_hbm, up_hbm)):
        for n, c in enumerate((core, 1 - core)):
            take = pl.ds(pl.multiple_of(c * half, half), half)
            place = cols_hbm.at[n * width : (n + 1) * width, k * half : (k + 1) * half]
            copies.append(pltpu.make_async_copy(w.at[:, take], place, sems.at[2 * k + n]))
    for c in copies:
        c.start()
    for c in copies:
        c.wait()


def dispatch_body(x_ref, y_ref, ids_ref, slot_ref, out_ref):
    code = ids_ref[...] * 64 + slot_ref[...]
    c0, c1, part = row_codes(out_ref.shape[0], 10 * lax.axis_index("xh"))

    def pick(c):
        hit = c == code[0:1, :]
        for k in range(1, code.shape[0]):
            hit = hit | (c == code[k : k + 1, :])
        return jnp.where(hit, 1.0, 0.0).astype(BF)

    def rows(p, ref):
        return jnp.dot(p, ref[...], preferred_element_type=F32)

    p0, p1 = pick(c0), pick(c1)
    out_ref[:, 0:256] = rows(p0, x_ref).astype(BF)
    out_ref[:, 256:512] = rows(p0, y_ref).astype(BF)
    tx, ty = rows(p1, x_ref), rows(p1, y_ref)
    tail = jnp.where(part == 0, tx[:, 0:128], tx[:, 128:256])
    tail2 = jnp.where(part == 2, ty[:, 0:128], ty[:, 128:256])
    out_ref[:, 512:640] = jnp.where(part < 2, tail, tail2).astype(BF)


def rows_of(a_ref, x_ref, t_ref):
    n = a_ref.shape[0]
    x_ref[0:n, :] = a_ref[:, 0:512]
    t_ref[...] = a_ref[:, 512:640].astype(F32)
    for g in range(4):
        x_ref[n:, g * 128 : (g + 1) * 128] = t_ref[pl.ds(g, n // 4, stride=4), :].astype(BF)


def up_body(a_ref, b_ref, waa_ref, wao_ref, wba_ref, wbo_ref, out_ref, xa, xb, ta, tb):
    rows_of(a_ref, xa, ta)
    rows_of(b_ref, xb, tb)

    @pl.loop(0, out_ref.shape[0] // 64)
    def _(i):
        s = pl.ds(pl.multiple_of(i * 64, 64), 64)
        t = None
        for x, w, k in (
            (xa, waa_ref, 0), (xa, wao_ref, 256), (xb, wba_ref, 0), (xb, wbo_ref, 256)
        ):
            v = jnp.dot(x[s, k : k + 256], w[0:256, :], preferred_element_type=F32)
            t = v if t is None else t + v
        out_ref[s, :] = t.astype(BF)


def act_body(p_ref, _, h_ref):
    rows = p_ref.shape[0] // 4
    half = h_ref.shape[1]

    @pl.loop(0, rows // 8)
    def _(i):
        def total(o):
            t = None
            for d in range(4):
                v = p_ref[pl.ds(pl.multiple_of(d * rows + i * 8, 8), 8), o : o + half]
                t = v.astype(F32) if t is None else t + v.astype(F32)
            return t

        g, u = total(0), total(half)
        h = (g / (1.0 + jnp.exp(-g)) * u).astype(BF)
        for d in range(4):
            h_ref[pl.ds(pl.multiple_of(d * rows + i * 8, 8), 8), :] = h


def down_body(ha_ref, hb_ref, w_ref, v0_ref, v1_ref, out_ref, h_ref, t_ref):
    n = out_ref.shape[0]
    half, cut = ha_ref.shape[1], v0_ref.shape[0]
    first = lax.axis_index("c") == 0
    ha, hb = ha_ref[...], hb_ref[...]
    h_ref[:, 0:half] = jnp.where(first, ha, hb)
    h_ref[:, half:] = jnp.where(first, hb, ha)

    def dot(h, m):
        return jnp.dot(h, m, preferred_element_type=F32)

    for k in range(2):
        if k == 0:
            t = dot(h_ref[...], w_ref[...])
        else:
            t = dot(h_ref[:, 0:cut], v0_ref[...]) + dot(h_ref[:, cut:], v1_ref[...])
        out_ref[:, k * 256 : (k + 1) * 256] = t[0:n].astype(BF)
        for g in range(2):
            t_ref[pl.ds(2 * k + g, n // 4, stride=4), :] = t[n:, g * 128 : (g + 1) * 128]
    out_ref[:, 512:640] = t_ref[...].astype(BF)


def combine_body(r_ref, ids_ref, slot_ref, w_ref, own_ref, send_ref):
    code = ids_ref[...] * 64 + slot_ref[...]
    w = w_ref[...]
    c0, c1, part = row_codes(r_ref.shape[0], 10 * lax.axis_index("xh"))

    def weights(c):
        t = jnp.where(c == code[0:1, :], w[0:1, :], 0.0)
        for k in range(1, code.shape[0]):
            t = t + jnp.where(c == code[k : k + 1, :], w[k : k + 1, :], 0.0)
        return t

    def mix(m, v):
        hi = m.astype(BF)
        lo = (m - hi.astype(F32)).astype(BF)
        dims = (((0,), (0,)), ((), ()))
        return lax.dot_general(hi, v, dims, preferred_element_type=F32) + lax.dot_general(
            lo, v, dims, preferred_element_type=F32
        )

    head, tail = weights(c0), weights(c1)
    v = r_ref[:, 512:640]
    for k, ref in ((0, own_ref), (1, send_ref)):
        t = mix(head, r_ref[:, k * 256 : (k + 1) * 256])
        for g in range(2):
            s = slice(g * 128, (g + 1) * 128)
            ref[:, s] = t[:, s] + mix(jnp.where(part == 2 * k + g, tail, 0.0), v)


def finish_body(own_ref, recv_ref, res_ref, out_ref):
    out_ref[...] = (res_ref[...].astype(F32) + own_ref[...] + recv_ref[...]).astype(BF)


def move(x, dx, dc):
    pairs = [(2 * h + c, 2 * ((h + dx) % 2) + (c + dc) % 2) for h in range(2) for c in range(2)]
    return lax.ppermute(x, ("xh", "c"), pairs)


def spread(x, axes):
    return lax.all_to_all(x, axes, split_axis=0, concat_axis=0, tiled=True)


def shards(tokens_in, residual, w_gate, w_up, w_down, expert_ids, slot_pos, route_weights):
    ids, slots, weights = expert_ids.T, slot_pos.T, route_weights.T
    width = tokens_in.shape[1]
    half = w_gate.shape[2] // 2
    sds = jax.ShapeDtypeStruct
    experts = lax.axis_size(E)
    rows = experts * 10
    chunks = sds((experts * 8, 640), BF)

    other_tokens = move(tokens_in, 1, 0)
    cols = call(
        columns_body,
        sds((2 * width, 2 * half), BF),
        w_gate[0], w_up[0],
        scratch=[pltpu.SemaphoreType.DMA((4,))],
        stay=range(2),
        name="columns",
    )
    cols_x = move(cols, 1, 0)
    w_c = move(cols[width:], 0, 1)
    w_xc = move(cols_x[width:], 0, 1)
    cut = half * 2 // 3
    down_first, down_last = move(w_down[0, :cut], 1, 0), move(w_down[0, cut:], 1, 0)
    outgoing = call(
        dispatch_body, chunks, tokens_in, other_tokens, ids, slots, name="dispatch"
    )
    arrived = spread(outgoing, E)
    arrived_b = move(arrived, 0, 1)
    partial = call(
        up_body,
        sds((rows, 2 * half), BF),
        arrived, arrived_b, cols, cols_x, w_c, w_xc,
        scratch=[pltpu.VMEM((rows, 512), BF)] * 2 + [pltpu.VMEM((experts * 8, 128), F32)] * 2,
        name="gate_up",
    )
    parts = spread(partial, "y")
    hidden = call(
        act_body, sds((rows, half), BF), parts, down_first, name="act"
    )
    hidden = spread(hidden, "y")
    hidden_b = move(hidden, 0, 1)
    result = call(
        down_body, chunks, hidden, hidden_b, w_down[0], down_first, down_last,
        scratch=[pltpu.VMEM((rows, 2 * half), BF), pltpu.VMEM((experts * 8, 128), F32)],
        name="down",
    )
    returned = spread(result, E)
    half_out = sds(tokens_in.shape, F32)
    own, send = call(
        combine_body, (half_out, half_out), returned, ids, slots, weights, name="combine"
    )
    recv = move(send, 1, 0)
    return call(finish_body, sds(tokens_in.shape, BF), own, recv, residual, name="finish")


def solution(mesh):
    fine = Mesh(mesh.devices.reshape(4, 2, 2, 16, 2), T + E)
    in_specs = (
        P(E, T),
        P(E, T),
        P(E, T, None),
        P(E, T, None),
        P(E, None, T),
        P(E, None),
        P(E, None),
        P(E, None),
    )
    return jax.shard_map(
        shards, mesh=fine, in_specs=in_specs, out_specs=P(E, T), check_vma=False
    )
```

time: 138 us -> 217 us (1.57)
  the two profiles are of different devices: /device:TPU:1 before, /device:TPU:2 now
where the time goes in v2:
time: 217 us; the launch traced here: 216 us
  waiting for transfers between devices  74.1 us (34%)
  Pallas kernels  58.7 us (27%)
  starting transfers between devices  52.3 us (24%)
  blocking collectives  26.2 us (12%)
  local copies, waits for them, and re-layouts  4.35 us (2%)
    pallas_call x7, Pallas kernels, call(): pl.pallas_call(body, out_shape=out, in_specs=[HBM if i in stay else VMEM...  58.7 us
    ppermute x9, waiting for transfers between devices, move(): return lax.ppermute(x, ('xh', 'c'), pairs)  51.5 us
    ppermute x9, starting transfers between devices, move(): return lax.ppermute(x, ('xh', 'c'), pairs)  27.6 us
    all_to_all x1, blocking collectives, spread(): return lax.all_to_all(x, axes, split_axis=0, concat_axis=0, tiled=True)  26.2 us
    all_to_all x3, starting transfers between devices, spread(): return lax.all_to_all(x, axes, split_axis=0, concat_axis=0, tiled=True)  24.8 us
    all_to_all x3, waiting for transfers between devices, spread(): return lax.all_to_all(x, axes, split_axis=0, concat_axis=0, tiled=True)  22.6 us
  transfers between devices with their start and end apart: 12, of which 8 were waited for; matrix products, arithmetic and copies ran while one was open for 2% of the time, Pallas kernels for 1%

profile of v2, /device:TPU:2, one launch (start us, length us, event | category | flops | bytes accessed | tf_op | source)
XLA Modules:
  0.0 216.0 jit_solution(12934846136792197072)
XLA Ops:
  0.0 0.0 copy-start.2
  0.0 0.0 copy-start.4
  0.0 0.0 copy-start.5
  0.0 48.8 %columns.1.waa_ref = bf16[512,1536]{1,0:T(8,128)(2,1)} custom-call(bf16[256,1536]{1,0:T(8,128)(2,1)} %bitcast.31, bf16[256,1536]{1,0:T(8,128)(2,1)} %bitcast.32), custom_call_target="tpu_custom_call" | custom-call | tf_op jit(solution)/shard_map/columns/pallas_call | solution.py:17
  48.8 4.0 %collective-permute-start.2 = (bf16[512,1536]{1,0:T(8,128)(2,1)}, bf16[512,1536]{1,0:T(8,128)(2,1)}, u32[]{:S(2)}, u32[]{:S(2)}) collective-permute-start(bf16[512,1536]{1,0:T(8,128)(2,1)} %columns.1.waa_ref), channel_id=1, source_target_pairs={{0,64},{32,96},{64,0},{96,32},{1,65},{33,97},{65,1},{97,33},{2,66}... | collective-permute-start | bytes 4718600 | tf_op jit(solution)/shard_map/ppermute | solution.py:172
  52.9 0.0 copy-done.2
  52.9 3.3 %collective-permute-start = (bf16[64,256]{1,0:T(8,128)(2,1)S(1)}, bf16[64,256]{1,0:T(8,128)(2,1)S(1)}, u32[]{:S(2)}, u32[]{:S(2)}) collective-permute-start(bf16[64,256]{1,0:T(8,128)(2,1)S(1)} %copy-done.2), channel_id=1, source_target_pairs={{0,64},{32,96},{64,0},{96,32},{1,65},{33,97},{65,1},{97,33},{2,66}... | collective-permute-start | bytes 98312 | tf_op jit(solution)/shard_map/ppermute | solution.py:172
  56.2 33.1 %collective-permute-done.y_ref = bf16[64,256]{1,0:T(8,128)(2,1)S(1)} collective-permute-done((bf16[64,256]{1,0:T(8,128)(2,1)S(1)}, bf16[64,256]{1,0:T(8,128)(2,1)S(1)}, u32[]{:S(2)}, u32[]{:S(2)}) %collective-permute-start) | collective-permute-done | bytes 32800 | tf_op jit(solution)/shard_map/ppermute | solution.py:172
  89.3 0.0 copy-done.4
  89.3 0.0 copy-done.5
  89.3 1.1 dispatch.1
  90.4 16.7 %all-to-all-start = ((bf16[32,8,640]{2,1,0:T(8,128)(2,1)}), bf16[32,8,640]{2,1,0:T(8,128)(2,1)S(1)}, u32[]{:S(2)}, u32[]{:S(2)}) async-start(bf16[32,8,640]{2,1,0:T(8,128)(2,1)} %bitcast.2), calls=%async_computation | async-start | bytes 655360 | tf_op jit(solution)/shard_map/all_to_all | solution.py:176
  107.1 0.0 copy-start
  107.1 2.2 %slice.16 = bf16[256,1536]{1,0:T(8,128)(2,1)} slice(bf16[512,1536]{1,0:T(8,128)(2,1)} %columns.1.waa_ref), slice={[256:512], [0:1536]} | slice | bytes 1572864 | tf_op jit(solution)/shard_map/slice | solution.py:198
  109.3 1.9 collective-permute-start.3
  111.2 0.0 collective-permute-done.2.wao_ref
  111.2 2.1 slice.17
  113.3 2.4 %collective-permute-start.4 = (bf16[256,1536]{1,0:T(8,128)(2,1)}, bf16[256,1536]{1,0:T(8,128)(2,1)S(1)}, u32[]{:S(2)}, u32[]{:S(2)}) collective-permute-start(bf16[256,1536]{1,0:T(8,128)(2,1)} %slice.17), channel_id=1, source_target_pairs={{0,32},{32,0},{64,96},{96,64},{1,33},{33,1},{65,97},{97,65},{2,34}... | collective-permute-start | bytes 2359304 | tf_op jit(solution)/shard_map/ppermute | solution.py:172
  115.7 15.0 %all-to-all-done = bf16[32,8,640]{2,1,0:T(8,128)(2,1)S(1)} async-done(((bf16[32,8,640]{2,1,0:T(8,128)(2,1)}), bf16[32,8,640]{2,1,0:T(8,128)(2,1)S(1)}, u32[]{:S(2)}, u32[]{:S(2)}) %all-to-all-start) | async-done | bytes 327712 | tf_op jit(solution)/shard_map/all_to_all | solution.py:176
  130.7 1.9 collective-permute-start.1
  132.6 0.0 collective-permute-done.3.wba_ref
  132.6 1.6 collective-permute-done.1.b_ref
  134.2 0.0 collective-permute-done.4.wbo_ref
  134.2 0.0 copy-done
  134.2 5.7 %gate_up.1 = bf16[320,1536]{1,0:T(8,128)(2,1)} custom-call(bf16[256,640]{1,0:T(8,128)(2,1)S(1)} %bitcast.23, bf16[256,640]{1,0:T(8,128)(2,1)S(1)} %collective-permute-done.1.b_ref, bf16[512,1536]{1,0:T(8,128)(2,1)S(1)} %copy-done, bf16[512,1536]{1,0:T(8,128)(2,1)} %collective-permute-done.2.wao_ref, bf16[256,1536]{1,0:T(8,128)(2,1)S(1)} %collective-permute-done.3.wba_ref, ...), custom_call_target="tpu_custom_call" | custom-call | tf_op jit(solution)/shard_map/gate_up/pallas_call | solution.py:17
  139.9 0.0 copy-start.1
  139.9 4.6 %all-to-all-start.1 = ((bf16[4,80,1536]{2,1,0:T(8,128)(2,1)}), bf16[4,80,1536]{2,1,0:T(8,128)(2,1)S(1)}, u32[]{:S(2)}, u32[]{:S(2)}) async-start(bf16[4,80,1536]{2,1,0:T(8,128)(2,1)} %bitcast.6), calls=%async_computation.1 | async-start | bytes 1966080 | tf_op jit(solution)/shard_map/all_to_all | solution.py:176
  144.5 0.0 copy-done.1
  144.6 4.0 %collective-permute-start.5 = (bf16[512,256]{1,0:T(8,128)(2,1)S(1)}, bf16[512,256]{1,0:T(8,128)(2,1)S(1)}, u32[]{:S(2)}, u32[]{:S(2)}) collective-permute-start(bf16[512,256]{1,0:T(8,128)(2,1)S(1)} %slice_bitcast_fusion.1), channel_id=1, source_target_pairs={{0,64},{32,96},{64,0},{96,32},{1,65},{33,97},{65,1},{97,33},{2,66}... | collective-permute-start | bytes 786440 | tf_op jit(solution)/shard_map/ppermute | solution.py:172
  148.6 7.4 %collective-permute-done.5._.v0_ref = bf16[512,256]{1,0:T(8,128)(2,1)S(1)} collective-permute-done((bf16[512,256]{1,0:T(8,128)(2,1)S(1)}, bf16[512,256]{1,0:T(8,128)(2,1)S(1)}, u32[]{:S(2)}, u32[]{:S(2)}) %collective-permute-start.5) | collective-permute-done | bytes 262176 | tf_op jit(solution)/shard_map/ppermute | solution.py:172
  156.0 3.2 %all-to-all-done.1 = bf16[4,80,1536]{2,1,0:T(8,128)(2,1)S(1)} async-done(((bf16[4,80,1536]{2,1,0:T(8,128)(2,1)}), bf16[4,80,1536]{2,1,0:T(8,128)(2,1)S(1)}, u32[]{:S(2)}, u32[]{:S(2)}) %all-to-all-start.1) | async-done | bytes 983072 | tf_op jit(solution)/shard_map/all_to_all | solution.py:176
  159.2 1.1 act.1
  160.4 3.5 %all-to-all-start.2 = ((bf16[4,80,768]{2,1,0:T(8,128)(2,1)}), bf16[4,80,768]{2,1,0:T(8,128)(2,1)S(1)}, u32[]{:S(2)}, u32[]{:S(2)}) async-start(bf16[4,80,768]{2,1,0:T(8,128)(2,1)} %bitcast.9), calls=%async_computation.2 | async-start | bytes 983040 | tf_op jit(solution)/shard_map/all_to_all | solution.py:176
  163.9 4.0 %collective-permute-start.7 = (bf16[1024,256]{1,0:T(8,128)(2,1)S(1)}, bf16[1024,256]{1,0:T(8,128)(2,1)S(1)}, u32[]{:S(2)}, u32[]{:S(2)}) collective-permute-start(bf16[1024,256]{1,0:T(8,128)(2,1)S(1)} %slice_bitcast_fusion), channel_id=1, source_target_pairs={{0,64},{32,96},{64,0},{96,32},{1,65},{33,97},{65,1},{97,33},{2,66}... | collective-permute-start | bytes 1572872 | tf_op jit(solution)/shard_map/ppermute | solution.py:172
  167.9 4.4 %all-to-all-done.2 = bf16[4,80,768]{2,1,0:T(8,128)(2,1)S(1)} async-done(((bf16[4,80,768]{2,1,0:T(8,128)(2,1)}), bf16[4,80,768]{2,1,0:T(8,128)(2,1)S(1)}, u32[]{:S(2)}, u32[]{:S(2)}) %all-to-all-start.2) | async-done | bytes 491552 | tf_op jit(solution)/shard_map/all_to_all | solution.py:176
  172.4 1.9 collective-permute-start.6
  174.3 5.8 %collective-permute-done.7.v1_ref = bf16[1024,256]{1,0:T(8,128)(2,1)S(1)} collective-permute-done((bf16[1024,256]{1,0:T(8,128)(2,1)S(1)}, bf16[1024,256]{1,0:T(8,128)(2,1)S(1)}, u32[]{:S(2)}, u32[]{:S(2)}) %collective-permute-start.7) | collective-permute-done | bytes 524320 | tf_op jit(solution)/shard_map/ppermute | solution.py:172
  180.1 0.0 collective-permute-done.6.hb_ref
  180.1 0.0 copy-start.6
  180.1 0.0 copy-start.3
  180.1 0.7 down.1
  180.8 26.2 %all_to_all.44 = bf16[32,8,640]{2,1,0:T(8,128)(2,1)S(1)} all-to-all(bf16[32,8,640]{2,1,0:T(8,128)(2,1)S(1)} %bitcast.25), channel_id=1, replica_groups=mesh['y'=4,'xh'=2,'c'=2,'z'=16,'xl'=2] {'z','xl'}, dimensions={0} | all-to-all | bytes 655360 | tf_op jit(solution)/shard_map/all_to_all | solution.py:176
  207.0 0.0 copy-done.6
  207.1 0.6 combine.1
  207.7 4.0 %collective-permute-start.8 = (f32[64,256]{1,0:T(8,128)S(1)}, f32[64,256]{1,0:T(8,128)S(1)}, u32[]{:S(2)}, u32[]{:S(2)}) collective-permute-start(f32[64,256]{1,0:T(8,128)S(1)} %get-tuple-element.8), channel_id=1, source_target_pairs={{0,64},{32,96},{64,0},{96,32},{1,65},{33,97},{65,1},{97,33},{2,66}... | collective-permute-start | bytes 196616 | tf_op jit(solution)/shard_map/ppermute | solution.py:172
  211.7 3.6 %collective-permute-done.8.recv_ref = f32[64,256]{1,0:T(8,128)S(1)} collective-permute-done((f32[64,256]{1,0:T(8,128)S(1)}, f32[64,256]{1,0:T(8,128)S(1)}, u32[]{:S(2)}, u32[]{:S(2)}) %collective-permute-start.8) | collective-permute-done | bytes 65568 | tf_op jit(solution)/shard_map/ppermute | solution.py:172
  215.3 0.0 copy-done.3
  215.3 0.6 finish.1
  (2 shorter events, 0.1 us)
Async XLA Ops:
  0.0 52.9 %copy-start.2 = (bf16[64,256]{1,0:T(8,128)(2,1)S(1)}, bf16[64,256]{1,0:T(8,128)(2,1)}, u32[]{:S(2)}) copy-start(bf16[64,256]{1,0:T(8,128)(2,1)} %x_ref.1) | copy-start | bytes 98308
  0.0 89.3 %copy-start.4 = (s32[64,8]{0,1:T(8,128)S(1)}, s32[64,8]{0,1:T(8,128)}, u32[]{:S(2)}) copy-start(s32[64,8]{0,1:T(8,128)} %param.13) | copy-start | bytes 6148
  0.0 89.3 %copy-start.5 = (s32[64,8]{0,1:T(8,128)S(1)}, s32[64,8]{0,1:T(8,128)}, u32[]{:S(2)}) copy-start(s32[64,8]{0,1:T(8,128)} %param.14) | copy-start | bytes 6148
  48.8 62.4 %collective-permute-start.2 = (bf16[512,1536]{1,0:T(8,128)(2,1)}, bf16[512,1536]{1,0:T(8,128)(2,1)}, u32[]{:S(2)}, u32[]{:S(2)}) collective-permute-start(bf16[512,1536]{1,0:T(8,128)(2,1)} %columns.1.waa_ref), channel_id=1, source_target_pairs={{0,64},{32,96},{64,0},{96,32},{1,65},{33,97},{65,1},{97,33},{2,66}... | collective-permute-start | bytes 4718600 | tf_op jit(solution)/shard_map/ppermute | solution.py:172
  52.9 36.4 %collective-permute-start = (bf16[64,256]{1,0:T(8,128)(2,1)S(1)}, bf16[64,256]{1,0:T(8,128)(2,1)S(1)}, u32[]{:S(2)}, u32[]{:S(2)}) collective-permute-start(bf16[64,256]{1,0:T(8,128)(2,1)S(1)} %copy-done.2), channel_id=1, source_target_pairs={{0,64},{32,96},{64,0},{96,32},{1,65},{33,97},{65,1},{97,33},{2,66}... | collective-permute-start | bytes 98312 | tf_op jit(solution)/shard_map/ppermute | solution.py:172
  90.4 40.3 %all-to-all-start = ((bf16[32,8,640]{2,1,0:T(8,128)(2,1)}), bf16[32,8,640]{2,1,0:T(8,128)(2,1)S(1)}, u32[]{:S(2)}, u32[]{:S(2)}) async-start(bf16[32,8,640]{2,1,0:T(8,128)(2,1)} %bitcast.2), calls=%async_computation | async-start | bytes 655360 | tf_op jit(solution)/shard_map/all_to_all | solution.py:176
  107.1 27.1 %copy-start = (bf16[512,1536]{1,0:T(8,128)(2,1)S(1)}, bf16[512,1536]{1,0:T(8,128)(2,1)}, u32[]{:S(2)}) copy-start(bf16[512,1536]{1,0:T(8,128)(2,1)} %columns.1.waa_ref) | copy-start | bytes 4718596
  109.3 23.3 %collective-permute-start.3 = (bf16[256,1536]{1,0:T(8,128)(2,1)}, bf16[256,1536]{1,0:T(8,128)(2,1)S(1)}, u32[]{:S(2)}, u32[]{:S(2)}) collective-permute-start(bf16[256,1536]{1,0:T(8,128)(2,1)} %slice.16), channel_id=1, source_target_pairs={{0,32},{32,0},{64,96},{96,64},{1,33},{33,1},{65,97},{97,65},{2,34}... | collective-permute-start | bytes 2359304 | tf_op jit(solution)/shard_map/ppermute | solution.py:172
  113.3 20.9 %collective-permute-start.4 = (bf16[256,1536]{1,0:T(8,128)(2,1)}, bf16[256,1536]{1,0:T(8,128)(2,1)S(1)}, u32[]{:S(2)}, u32[]{:S(2)}) collective-permute-start(bf16[256,1536]{1,0:T(8,128)(2,1)} %slice.17), channel_id=1, source_target_pairs={{0,32},{32,0},{64,96},{96,64},{1,33},{33,1},{65,97},{97,65},{2,34}... | collective-permute-start | bytes 2359304 | tf_op jit(solution)/shard_map/ppermute | solution.py:172
  130.7 3.5 %collective-permute-start.1 = (bf16[256,640]{1,0:T(8,128)(2,1)S(1)}, bf16[256,640]{1,0:T(8,128)(2,1)S(1)}, u32[]{:S(2)}, u32[]{:S(2)}) collective-permute-start(bf16[256,640]{1,0:T(8,128)(2,1)S(1)} %bitcast.22), channel_id=1, source_target_pairs={{0,32},{32,0},{64,96},{96,64},{1,33},{33,1},{65,97},{97,65},{2,34}... | collective-permute-start | bytes 983048 | tf_op jit(solution)/shard_map/ppermute | solution.py:172
  139.9 4.6 %copy-start.1 = (bf16[1,1536,256]{2,1,0:T(8,128)(2,1)S(1)}, bf16[1,1536,256]{2,1,0:T(8,128)(2,1)}, u32[]{:S(2)}) copy-start(bf16[1,1536,256]{2,1,0:T(8,128)(2,1)} %param.12) | copy-start | bytes 2359300
  139.9 19.3 %all-to-all-start.1 = ((bf16[4,80,1536]{2,1,0:T(8,128)(2,1)}), bf16[4,80,1536]{2,1,0:T(8,128)(2,1)S(1)}, u32[]{:S(2)}, u32[]{:S(2)}) async-start(bf16[4,80,1536]{2,1,0:T(8,128)(2,1)} %bitcast.6), calls=%async_computation.1 | async-start | bytes 1966080 | tf_op jit(solution)/shard_map/all_to_all | solution.py:176
  144.6 11.5 %collective-permute-start.5 = (bf16[512,256]{1,0:T(8,128)(2,1)S(1)}, bf16[512,256]{1,0:T(8,128)(2,1)S(1)}, u32[]{:S(2)}, u32[]{:S(2)}) collective-permute-start(bf16[512,256]{1,0:T(8,128)(2,1)S(1)} %slice_bitcast_fusion.1), channel_id=1, source_target_pairs={{0,64},{32,96},{64,0},{96,32},{1,65},{33,97},{65,1},{97,33},{2,66}... | collective-permute-start | bytes 786440 | tf_op jit(solution)/shard_map/ppermute | solution.py:172
  160.4 12.0 %all-to-all-start.2 = ((bf16[4,80,768]{2,1,0:T(8,128)(2,1)}), bf16[4,80,768]{2,1,0:T(8,128)(2,1)S(1)}, u32[]{:S(2)}, u32[]{:S(2)}) async-start(bf16[4,80,768]{2,1,0:T(8,128)(2,1)} %bitcast.9), calls=%async_computation.2 | async-start | bytes 983040 | tf_op jit(solution)/shard_map/all_to_all | solution.py:176
  163.9 16.2 %collective-permute-start.7 = (bf16[1024,256]{1,0:T(8,128)(2,1)S(1)}, bf16[1024,256]{1,0:T(8,128)(2,1)S(1)}, u32[]{:S(2)}, u32[]{:S(2)}) collective-permute-start(bf16[1024,256]{1,0:T(8,128)(2,1)S(1)} %slice_bitcast_fusion), channel_id=1, source_target_pairs={{0,64},{32,96},{64,0},{96,32},{1,65},{33,97},{65,1},{97,33},{2,66}... | collective-permute-start | bytes 1572872 | tf_op jit(solution)/shard_map/ppermute | solution.py:172
  172.4 7.7 %collective-permute-start.6 = (bf16[320,768]{1,0:T(8,128)(2,1)S(1)}, bf16[320,768]{1,0:T(8,128)(2,1)S(1)}, u32[]{:S(2)}, u32[]{:S(2)}) collective-permute-start(bf16[320,768]{1,0:T(8,128)(2,1)S(1)} %bitcast.20), channel_id=1, source_target_pairs={{0,32},{32,0},{64,96},{96,64},{1,33},{33,1},{65,97},{97,65},{2,34}... | collective-permute-start | bytes 1474568 | tf_op jit(solution)/shard_map/ppermute | solution.py:172
  180.1 26.9 %copy-start.6 = (f32[64,8]{0,1:T(8,128)S(1)}, f32[64,8]{0,1:T(8,128)}, u32[]{:S(2)}) copy-start(f32[64,8]{0,1:T(8,128)} %param.15) | copy-start | bytes 6148
  180.1 35.2 %copy-start.3 = (bf16[64,256]{1,0:T(8,128)(2,1)S(1)}, bf16[64,256]{1,0:T(8,128)(2,1)}, u32[]{:S(2)}) copy-start(bf16[64,256]{1,0:T(8,128)(2,1)} %res_ref.1) | copy-start | bytes 98308
  207.7 7.7 %collective-permute-start.8 = (f32[64,256]{1,0:T(8,128)S(1)}, f32[64,256]{1,0:T(8,128)S(1)}, u32[]{:S(2)}, u32[]{:S(2)}) collective-permute-start(f32[64,256]{1,0:T(8,128)S(1)} %get-tuple-element.8), channel_id=1, source_target_pairs={{0,64},{32,96},{64,0},{96,32},{1,65},{33,97},{65,1},{97,33},{2,66}... | collective-permute-start | bytes 196616 | tf_op jit(solution)/shard_map/ppermute | solution.py:172

commit v3 on v1

--- a/solution.py
+++ b/solution.py
@@ -1,5 +1,3 @@
-import functools
-
 import jax
 import jax.numpy as jnp
 from jax import lax
@@ -13,16 +11,17 @@
 R = ("y", "xh")
 E = ("z", "xl")
 VMEM = pl.BlockSpec(memory_space=pltpu.VMEM)
-
-
-def call(body, out, *args, name, limit=48 << 20, scratch=(), flops=0, moved=0):
+HBM = pl.BlockSpec(memory_space=pltpu.HBM)
+
+
+def call(body, out, *args, name, limit=48 << 20, scratch=(), flops=0, moved=0, stay=()):
     return pl.pallas_call(
         body,
         out_shape=out,
-        in_specs=[VMEM] * len(args),
+        in_specs=[HBM if i in stay else VMEM for i in range(len(args))],
         out_specs=jax.tree.map(lambda _: VMEM, out),
         scratch_shapes=list(scratch),
-        compiler_params=pltpu.CompilerParams(vmem_limit_bytes=limit),
+        compiler_params=pltpu.CompilerParams(vmem_limit_bytes=None if stay else limit),
         cost_estimate=pl.CostEstimate(flops=flops, bytes_accessed=moved, transcendentals=0),
         name=name,
     )(*args)
@@ -35,10 +34,18 @@
     return base + j, base + 8 + j, base + 16 + lax.rem(j, 4), j < 4
 
 
-def dispatch_body(x_ref, ids_ref, slot_ref, out_ref):
+def dispatch_body(x_hbm, ids_hbm, slot_hbm, out_ref, x_ref, ids_ref, slot_ref, sems):
+    copies = [
+        pltpu.make_async_copy(a, b, sems.at[i])
+        for i, (a, b) in enumerate(((ids_hbm, ids_ref), (slot_hbm, slot_ref), (x_hbm, x_ref)))
+    ]
+    for c in copies:
+        c.start()
+    c0, c1, c2, low = row_codes(out_ref.shape[0])
+    for c in copies:
+        c.wait()
     code = ids_ref[...] * 64 + slot_ref[...]
     x = x_ref[...]
-    c0, c1, c2, low = row_codes(out_ref.shape[0])
 
     def pick(c):
         hit = c == code[0:1, :]
@@ -67,9 +74,11 @@
     x_ref[2 * n :, 128:256] = b1.reshape(n // 2, 128).astype(BF)
 
 
-def up_body(a_ref, b_ref, wga_ref, wgb_ref, wua_ref, wub_ref, out_ref, xa, xb):
-    rows_of(a_ref, xa)
-    rows_of(b_ref, xb)
+def up_body(x_ref, wga_ref, wgb_ref, wua_ref, wub_ref, _, out_ref, xa, xb):
+    n = x_ref.shape[0] // 2
+    core = lax.axis_index("c")
+    rows_of(x_ref.at[pl.ds(pl.multiple_of(core * n, n), n)], xa)
+    rows_of(x_ref.at[pl.ds(pl.multiple_of((1 - core) * n, n), n)], xb)
     half = wga_ref.shape[1]
 
     @pl.loop(0, out_ref.shape[0] // 128)
@@ -121,10 +130,11 @@
     out_ref[:, 512:640] = jnp.stack([t0, t1], axis=1).reshape(n, 128).astype(BF)
 
 
-def combine_body(r_ref, res_ref, ids_ref, slot_ref, w_ref, out_ref):
+def weigh_body(ids_ref, slot_ref, w_ref, out_ref):
     code = ids_ref[...] * 64 + slot_ref[...]
     w = w_ref[...]
-    c0, c1, c2, low = row_codes(r_ref.shape[0])
+    rows = out_ref.shape[1]
+    c0, c1, c2, low = row_codes(rows)
 
     def weights(c):
         t = jnp.where(c == code[0:1, :], w[0:1, :], 0.0)
@@ -132,20 +142,27 @@
             t = t + jnp.where(c == code[k : k + 1, :], w[k : k + 1, :], 0.0)
         return t
 
-    def mix(m, v):
+    tail = weights(c2)
+    sets = (weights(c0), weights(c1), jnp.where(low, tail, 0.0), jnp.where(low, 0.0, tail))
+    for k, m in enumerate(sets):
+        m = jnp.transpose(m)
         hi = m.astype(BF)
-        lo = (m - hi.astype(F32)).astype(BF)
-        dims = (((0,), (0,)), ((), ()))
-        return lax.dot_general(hi, v, dims, preferred_element_type=F32) + lax.dot_general(
-            lo, v, dims, preferred_element_type=F32
-        )
-
-    total = res_ref[...].astype(F32)
-    total += mix(weights(c0), r_ref[:, 0:256]) + mix(weights(c1), r_ref[:, 256:512])
-    tail = weights(c2)
+        n = m.shape[0]
+        out_ref[2 * k * n : (2 * k + 1) * n, :] = hi
+        out_ref[(2 * k + 1) * n : (2 * k + 2) * n, :] = (m - hi.astype(F32)).astype(BF)
+
+
+def combine_body(r_ref, res_ref, m_ref, out_ref):
+    n = res_ref.shape[0]
+
+    def mix(k, v):
+        t = jnp.dot(m_ref[2 * k * n : (2 * k + 2) * n, :], v, preferred_element_type=F32)
+        return t[0:n] + t[n:]
+
+    total = res_ref[...].astype(F32) + mix(0, r_ref[:, 0:256]) + mix(1, r_ref[:, 256:512])
     v = r_ref[:, 512:640]
-    out_ref[:, 0:128] = (total[:, 0:128] + mix(jnp.where(low, tail, 0.0), v)).astype(BF)
-    out_ref[:, 128:256] = (total[:, 128:256] + mix(jnp.where(low, 0.0, tail), v)).astype(BF)
+    out_ref[:, 0:128] = (total[:, 0:128] + mix(2, v)).astype(BF)
+    out_ref[:, 128:256] = (total[:, 128:256] + mix(3, v)).astype(BF)
 
 
 def swap(x):
@@ -170,17 +187,28 @@
         return mine, other
 
     outgoing = call(
-        dispatch_body, sds((experts * 8, 640), BF), tokens_in, ids, slots, name="dispatch"
+        dispatch_body, sds((experts * 8, 640), BF), tokens_in, ids, slots,
+        scratch=[
+            pltpu.VMEM(tokens_in.shape, BF),
+            pltpu.VMEM(ids.shape, jnp.int32),
+            pltpu.VMEM(ids.shape, jnp.int32),
+            pltpu.SemaphoreType.DMA((3,)),
+        ],
+        stay=range(3),
+        name="dispatch",
+    )
+    mixing = call(
+        weigh_body, sds((8 * ids.shape[1], experts * 8), BF), ids, slots, weights, name="weigh"
     )
     gate_mine, gate_other = halves(w_gate[0], 1)
     up_mine, up_other = halves(w_up[0], 1)
     gate_recv, up_recv = swap(gate_other), swap(up_other)
     arrived = spread(outgoing, E)
-    arrived_b = swap(arrived)
+    arrived = lax.all_gather(arrived, "c", axis=0, tiled=True)
     partial = call(
         up_body,
         sds((rows, 2 * half), BF),
-        arrived, arrived_b, gate_mine, gate_recv, up_mine, up_recv,
+        arrived, gate_mine, gate_recv, up_mine, up_recv, mixing,
         scratch=[pltpu.VMEM((rows, 256), BF)] * 2,
         name="gate_up",
     )
@@ -195,8 +223,7 @@
     )
     returned = spread(result, E)
     return call(
-        combine_body, sds(tokens_in.shape, BF), returned, residual, ids, slots, weights,
-        name="combine",
+        combine_body, sds(tokens_in.shape, BF), returned, residual, mixing, name="combine"
     )
 
 

time: 138 us -> 135 us (0.978)
  blocking collectives: 77 us -> 81.4 us
  starting transfers between devices: 30.6 us -> 26.5 us
  waiting for transfers between devices: 20.5 us -> 18.1 us
  local copies, waits for them, and re-layouts: 3.46 us -> 2.07 us
    ppermute x4 -> x3, starting transfers between devices: 13.6 us -> 9.38 us  [swap(): return lax.ppermute(x, 'c', [(0, 1), (1, 0)])]
    all_gather x0 -> x1, blocking collectives: none -> 4.26 us  [shards(): arrived = lax.all_gather(arrived, 'c', axis=0, tiled=True)]
    unnamed x18 -> x12, local copies, waits for them, and re-layouts: 2.16 us -> 0.03 us
    ppermute x4 -> x3, waiting for transfers between devices: 3.26 us -> 2.09 us  [swap(): return lax.ppermute(x, 'c', [(0, 1), (1, 0)])]
    pallas_call x5 -> x6, Pallas kernels: 5.53 us -> 6.47 us  [call(): pl.pallas_call(body, out_shape=out, in_specs=[HBM if i in stay else VMEM...]
  transfers between devices with their start and end apart: 5 -> 4, of which waited for: 3 -> 2; matrix products, arithmetic and copies ran while one was open for 1% -> 2% of each run, Pallas kernels for 0% -> 0%
where the time goes in v3:
time: 135 us
  blocking collectives  81.4 us (60%)
  starting transfers between devices  26.5 us (20%)
  waiting for transfers between devices  18.1 us (13%)
  Pallas kernels  6.47 us (5%)
  local copies, waits for them, and re-layouts  2.07 us (2%)
    all_to_all x3, blocking collectives, spread(): return lax.all_to_all(x, axes, split_axis=0, concat_axis=0, tiled=True)  77.1 us
    all_to_all x1, starting transfers between devices, spread(): return lax.all_to_all(x, axes, split_axis=0, concat_axis=0, tiled=True)  17.1 us
    all_to_all x1, waiting for transfers between devices, spread(): return lax.all_to_all(x, axes, split_axis=0, concat_axis=0, tiled=True)  16 us
    ppermute x3, starting transfers between devices, swap(): return lax.ppermute(x, 'c', [(0, 1), (1, 0)])  9.38 us
    pallas_call x6, Pallas kernels, call(): pl.pallas_call(body, out_shape=out, in_specs=[HBM if i in stay else VMEM...  6.47 us
    all_gather x1, blocking collectives, shards(): arrived = lax.all_gather(arrived, 'c', axis=0, tiled=True)  4.26 us
  transfers between devices with their start and end apart: 4, of which 2 were waited for; matrix products, arithmetic and copies ran while one was open for 2% of the time, Pallas kernels for 0%

profile of v3, /device:TPU:1, one launch (start us, length us, event | category | flops | bytes accessed | tf_op | source)
XLA Modules:
  0.0 134.6 jit_solution(13517013220166360095)
XLA Ops:
  0.0 0.0 copy-start.4
  0.0 2.1 %dispatch.1 = bf16[256,640]{1,0:T(8,128)(2,1)} custom-call(bf16[64,256]{1,0:T(8,128)(2,1)} %x_hbm.1, s32[8,64]{1,0:T(8,128)} %bitcast.30, s32[8,64]{1,0:T(8,128)} %bitcast.32), custom_call_target="tpu_custom_call" | custom-call | tf_op jit(solution)/shard_map/dispatch/pallas_call | solution.py:18
  2.1 0.0 copy-start.1
  2.1 0.0 copy-start.2
  2.1 0.0 copy-start.3
  2.1 17.1 %all-to-all-start = ((bf16[32,8,640]{2,1,0:T(8,128)(2,1)}), bf16[32,8,640]{2,1,0:T(8,128)(2,1)S(1)}, u32[]{:S(2)}, u32[]{:S(2)}) async-start(bf16[32,8,640]{2,1,0:T(8,128)(2,1)} %bitcast.35), calls=%async_computation | async-start | bytes 655360 | tf_op jit(solution)/shard_map/all_to_all | solution.py:173
  19.3 1.2 dynamic-slice_bitcast_fusion.4
  20.4 2.9 %collective-permute-start = (bf16[256,768]{1,0:T(8,128)(2,1)S(1)}, bf16[256,768]{1,0:T(8,128)(2,1)S(1)}, u32[]{:S(2)}, u32[]{:S(2)}) collective-permute-start(bf16[256,768]{1,0:T(8,128)(2,1)S(1)} %get-tuple-element.9), channel_id=1, source_target_pairs={{0,32},{32,0},{1,33},{33,1},{2,34},{34,2},{3,35},{35,3},{4,36},{36... | collective-permute-start | bytes 1179656 | tf_op jit(solution)/shard_map/ppermute | solution.py:169
  23.3 0.0 copy-done.4
  23.3 0.8 dynamic-slice_bitcast_fusion.2
  24.1 1.9 %collective-permute-start.1 = (bf16[256,768]{1,0:T(8,128)(2,1)}, bf16[256,768]{1,0:T(8,128)(2,1)S(1)}, u32[]{:S(2)}, u32[]{:S(2)}) collective-permute-start(bf16[256,768]{1,0:T(8,128)(2,1)} %get-tuple-element.7), channel_id=1, source_target_pairs={{0,32},{32,0},{1,33},{33,1},{2,34},{34,2},{3,35},{35,3},{4,36},{36... | collective-permute-start | bytes 1179656 | tf_op jit(solution)/shard_map/ppermute | solution.py:169
  26.0 0.0 copy-done.1
  26.0 0.0 copy-done.2
  26.0 0.0 copy-done.3
  26.1 0.5 weigh.1._.m_ref
  26.5 16.0 %all-to-all-done = bf16[32,8,640]{2,1,0:T(8,128)(2,1)S(1)} async-done(((bf16[32,8,640]{2,1,0:T(8,128)(2,1)}), bf16[32,8,640]{2,1,0:T(8,128)(2,1)S(1)}, u32[]{:S(2)}, u32[]{:S(2)}) %all-to-all-start) | async-done | bytes 327712 | tf_op jit(solution)/shard_map/all_to_all | solution.py:173
  42.5 4.3 %all_gather.3.x_ref = bf16[512,640]{1,0:T(8,128)(2,1)S(1)} all-gather(bf16[256,640]{1,0:T(8,128)(2,1)S(1)} %bitcast.36), channel_id=1, replica_groups=mesh['y'=4,'xh'=2,'c'=2,'z'=16,'xl'=2] {'c'}, dimensions={0}, use_global_device_ids=true | all-gather | bytes 983040 | tf_op jit(solution)/shard_map/all_gather | solution.py:207
  46.8 0.0 collective-permute-done.wgb_ref
  46.8 0.0 collective-permute-done.1.wub_ref
  46.8 2.0 %gate_up.1 = bf16[640,1536]{1,0:T(8,128)(2,1)S(1)} custom-call(bf16[512,640]{1,0:T(8,128)(2,1)S(1)} %all_gather.3.x_ref, bf16[256,768]{1,0:T(8,128)(2,1)S(1)} %get-tuple-element.10.wga_ref, bf16[256,768]{1,0:T(8,128)(2,1)S(1)} %collective-permute-done.wgb_ref, bf16[256,768]{1,0:T(8,128)(2,1)S(1)} %get-tuple-element.8.wua_ref, ...), custom_call_target="tpu_custom_call" | custom-call | tf_op jit(solution)/shard_map/gate_up/pallas_call | solution.py:18
  48.7 32.4 %all_to_all.45 = bf16[8,80,1536]{2,1,0:T(8,128)(2,1)S(1)} all-to-all(bf16[8,80,1536]{2,1,0:T(8,128)(2,1)S(1)} %bitcast.23), channel_id=1, replica_groups=mesh['y'=4,'xh'=2,'c'=2,'z'=16,'xl'=2] {'y','xh'}, dimensions={0} | all-to-all | bytes 3932160 | tf_op jit(solution)/shard_map/all_to_all | solution.py:173
  81.1 0.0 copy-start.5
  81.1 0.4 act.1
  81.5 17.6 %all_to_all.46 = bf16[8,80,768]{2,1,0:T(8,128)(2,1)S(1)} all-to-all(bf16[8,80,768]{2,1,0:T(8,128)(2,1)S(1)} %bitcast.27), channel_id=1, replica_groups=mesh['y'=4,'xh'=2,'c'=2,'z'=16,'xl'=2] {'y','xh'}, dimensions={0} | all-to-all | bytes 1966080 | tf_op jit(solution)/shard_map/all_to_all | solution.py:173
  99.2 4.6 %collective-permute-start.2 = (bf16[640,768]{1,0:T(8,128)(2,1)S(1)}, bf16[640,768]{1,0:T(8,128)(2,1)S(1)}, u32[]{:S(2)}, u32[]{:S(2)}) collective-permute-start(bf16[640,768]{1,0:T(8,128)(2,1)S(1)} %bitcast.25), channel_id=1, source_target_pairs={{0,32},{32,0},{1,33},{33,1},{2,34},{34,2},{3,35},{35,3},{4,36},{36... | collective-permute-start | bytes 2949128 | tf_op jit(solution)/shard_map/ppermute | solution.py:169
  103.8 0.0 copy-done.5
  103.8 0.1 dynamic-slice_bitcast_fusion
  103.9 0.0 copy-start
  103.9 2.1 %collective-permute-done.2.hb_ref = bf16[640,768]{1,0:T(8,128)(2,1)S(1)} collective-permute-done((bf16[640,768]{1,0:T(8,128)(2,1)S(1)}, bf16[640,768]{1,0:T(8,128)(2,1)S(1)}, u32[]{:S(2)}, u32[]{:S(2)}) %collective-permute-start.2) | collective-permute-done | bytes 983072 | tf_op jit(solution)/shard_map/ppermute | solution.py:169
  105.9 0.7 down.1
  106.6 27.1 %all_to_all.47 = bf16[32,8,640]{2,1,0:T(8,128)(2,1)S(1)} all-to-all(bf16[32,8,640]{2,1,0:T(8,128)(2,1)S(1)} %bitcast.28), channel_id=1, replica_groups=mesh['y'=4,'xh'=2,'c'=2,'z'=16,'xl'=2] {'z','xl'}, dimensions={0} | all-to-all | bytes 655360 | tf_op jit(solution)/shard_map/all_to_all | solution.py:173
  133.8 0.0 copy-done
  133.8 0.8 combine.1
Async XLA Ops:
  0.0 23.3 %copy-start.4 = (bf16[1,256,1536]{2,1,0:T(8,128)(2,1)S(1)}, bf16[1,256,1536]{2,1,0:T(8,128)(2,1)}, u32[]{:S(2)}) copy-start(bf16[1,256,1536]{2,1,0:T(8,128)(2,1)} %param.11) | copy-start | bytes 2359300
  2.1 23.9 %copy-start.1 = (s32[64,8]{0,1:T(8,128)S(1)}, s32[64,8]{0,1:T(8,128)}, u32[]{:S(2)}) copy-start(s32[64,8]{0,1:T(8,128)} %param.13) | copy-start | bytes 6148
  2.1 23.9 %copy-start.2 = (s32[64,8]{0,1:T(8,128)S(1)}, s32[64,8]{0,1:T(8,128)}, u32[]{:S(2)}) copy-start(s32[64,8]{0,1:T(8,128)} %param.14) | copy-start | bytes 6148
  2.1 23.9 %copy-start.3 = (f32[64,8]{0,1:T(8,128)S(1)}, f32[64,8]{0,1:T(8,128)}, u32[]{:S(2)}) copy-start(f32[64,8]{0,1:T(8,128)} %param.15) | copy-start | bytes 6148
  2.1 40.4 %all-to-all-start = ((bf16[32,8,640]{2,1,0:T(8,128)(2,1)}), bf16[32,8,640]{2,1,0:T(8,128)(2,1)S(1)}, u32[]{:S(2)}, u32[]{:S(2)}) async-start(bf16[32,8,640]{2,1,0:T(8,128)(2,1)} %bitcast.35), calls=%async_computation | async-start | bytes 655360 | tf_op jit(solution)/shard_map/all_to_all | solution.py:173
  20.4 26.3 %collective-permute-start = (bf16[256,768]{1,0:T(8,128)(2,1)S(1)}, bf16[256,768]{1,0:T(8,128)(2,1)S(1)}, u32[]{:S(2)}, u32[]{:S(2)}) collective-permute-start(bf16[256,768]{1,0:T(8,128)(2,1)S(1)} %get-tuple-element.9), channel_id=1, source_target_pairs={{0,32},{32,0},{1,33},{33,1},{2,34},{34,2},{3,35},{35,3},{4,36},{36... | collective-permute-start | bytes 1179656 | tf_op jit(solution)/shard_map/ppermute | solution.py:169
  24.1 22.6 %collective-permute-start.1 = (bf16[256,768]{1,0:T(8,128)(2,1)}, bf16[256,768]{1,0:T(8,128)(2,1)S(1)}, u32[]{:S(2)}, u32[]{:S(2)}) collective-permute-start(bf16[256,768]{1,0:T(8,128)(2,1)} %get-tuple-element.7), channel_id=1, source_target_pairs={{0,32},{32,0},{1,33},{33,1},{2,34},{34,2},{3,35},{35,3},{4,36},{36... | collective-permute-start | bytes 1179656 | tf_op jit(solution)/shard_map/ppermute | solution.py:169
  81.1 22.7 %copy-start.5 = (bf16[1,1536,256]{2,1,0:T(8,128)(2,1)S(1)}, bf16[1,1536,256]{2,1,0:T(8,128)(2,1)}, u32[]{:S(2)}) copy-start(bf16[1,1536,256]{2,1,0:T(8,128)(2,1)} %param.12) | copy-start | bytes 2359300
  99.2 6.8 %collective-permute-start.2 = (bf16[640,768]{1,0:T(8,128)(2,1)S(1)}, bf16[640,768]{1,0:T(8,128)(2,1)S(1)}, u32[]{:S(2)}, u32[]{:S(2)}) collective-permute-start(bf16[640,768]{1,0:T(8,128)(2,1)S(1)} %bitcast.25), channel_id=1, source_target_pairs={{0,32},{32,0},{1,33},{33,1},{2,34},{34,2},{3,35},{35,3},{4,36},{36... | collective-permute-start | bytes 2949128 | tf_op jit(solution)/shard_map/ppermute | solution.py:169
  103.9 29.9 %copy-start = (bf16[64,256]{1,0:T(8,128)(2,1)S(1)}, bf16[64,256]{1,0:T(8,128)(2,1)}, u32[]{:S(2)}) copy-start(bf16[64,256]{1,0:T(8,128)(2,1)} %res_ref.1) | copy-start | bytes 98308

commit v4 on v3

v4 whole, which is shorter than its diff:
```python
import jax
import jax.numpy as jnp
from jax import lax
from jax.experimental import pallas as pl
from jax.experimental.pallas import tpu as pltpu
from jax.sharding import Mesh, PartitionSpec as P

BF = jnp.bfloat16
F32 = jnp.float32
T = ("y", "xh", "c")
R = ("y", "xh")
E = ("z", "xl")
LINE = ("xl", "z")
VMEM = pl.BlockSpec(memory_space=pltpu.VMEM)
HBM = pl.BlockSpec(memory_space=pltpu.HBM)


def call(body, out, *args, name, limit=16 << 20, scratch=(), stay=False):
    return pl.pallas_call(
        body,
        out_shape=out,
        in_specs=[HBM if stay else VMEM] * len(args),
        out_specs=jax.tree.map(lambda _: VMEM, out),
        scratch_shapes=list(scratch),
        compiler_params=pltpu.CompilerParams(vmem_limit_bytes=None if stay else limit),
        name=name,
    )(*args)


def row_codes(rows, first):
    r = lax.broadcasted_iota(jnp.int32, (rows, 1), 0)
    d, j = r // 8, lax.rem(r, 8)
    experts = rows // 8
    base = (lax.rem(d, experts // 2) * 2 + d // (experts // 2)) * 64 + first
    return base + j, base + 8 + j // 4, lax.rem(j, 4)


def part_of(ref, index, count):
    return ref[pl.ds(pl.multiple_of(index * count, count), count), :]


def dispatch_body(x_hbm, ids_hbm, slot_hbm, out_ref, x_ref, ids_ref, slot_ref, sems):
    copies = [
        pltpu.make_async_copy(a, b, sems.at[i])
        for i, (a, b) in enumerate(((ids_hbm, ids_ref), (slot_hbm, slot_ref), (x_hbm, x_ref)))
    ]
    for c in copies:
        c.start()
    core = lax.axis_index("c")
    n = x_ref.shape[0] // 2
    c0, c1, part = row_codes(out_ref.shape[0], 10 * core)
    for c in copies:
        c.wait()
    code = ids_ref[...] * 64 + slot_ref[...]
    own, other = part_of(x_ref, core, n), part_of(x_ref, 1 - core, n)

    def pick(c):
        hit = c == code[0:1, :]
        for k in range(1, code.shape[0]):
            hit = hit | (c == code[k : k + 1, :])
        return jnp.where(hit, 1.0, 0.0).astype(BF)

    def rows(p, x):
        return jnp.dot(p, x, preferred_element_type=F32)

    p0, p1 = pick(c0), pick(c1)
    out_ref[:, 0:256] = rows(p0, own).astype(BF)
    out_ref[:, 256:512] = rows(p0, other).astype(BF)
    tx, ty = rows(p1, own), rows(p1, other)
    tail = jnp.where(part == 0, tx[:, 0:128], tx[:, 128:256])
    tail2 = jnp.where(part == 2, ty[:, 0:128], ty[:, 128:256])
    out_ref[:, 512:640] = jnp.where(part < 2, tail, tail2).astype(BF)


def stack_body(ga_ref, gb_ref, ua_ref, ub_ref, _, __, out_ref):
    k, half = ga_ref.shape
    out_ref[0:k, 0:half] = ga_ref[...]
    out_ref[k:, 0:half] = gb_ref[...]
    out_ref[0:k, half:] = ua_ref[...]
    out_ref[k:, half:] = ub_ref[...]


def up_body(a_ref, w_ref, out_ref, x_ref, t_ref):
    n = a_ref.shape[0]
    x_ref[0:n, :] = a_ref[:, 0:512]
    t_ref[...] = a_ref[:, 512:640].astype(F32)
    for g in range(4):
        x_ref[n:, g * 128 : (g + 1) * 128] = t_ref[pl.ds(g, n // 4, stride=4), :].astype(BF)

    @pl.loop(0, out_ref.shape[0] // 64)
    def _(i):
        s = pl.ds(pl.multiple_of(i * 64, 64), 64)
        out_ref[s, :] = jnp.dot(x_ref[s, :], w_ref[...], preferred_element_type=F32).astype(BF)


def act_body(p_ref, h_ref):
    rows = p_ref.shape[0] // 8
    half = h_ref.shape[1]

    @pl.loop(0, rows // 8)
    def _(i):
        def total(o):
            t = None
            for d in range(8):
                v = p_ref[pl.ds(pl.multiple_of(d * rows + i * 8, 8), 8), o : o + half]
                t = v.astype(F32) if t is None else t + v.astype(F32)
            return t

        g, u = total(0), total(half)
        h = (g / (1.0 + jnp.exp(-g)) * u).astype(BF)
        for d in range(8):
            h_ref[pl.ds(pl.multiple_of(d * rows + i * 8, 8), 8), :] = h


def down_body(h_ref, w_ref, v_ref, out_ref, t_ref):
    n = out_ref.shape[0]
    for k, m in ((0, w_ref), (1, v_ref)):
        t = jnp.dot(h_ref[...], m[...], preferred_element_type=F32)
        out_ref[:, k * 256 : (k + 1) * 256] = t[0:n].astype(BF)
        for g in range(2):
            t_ref[pl.ds(2 * k + g, n // 4, stride=4), :] = t[n:, g * 128 : (g + 1) * 128]
    out_ref[:, 512:640] = t_ref[...].astype(BF)


def weigh_body(ids_ref, slot_ref, w_ref, out_ref):
    code = ids_ref[...] * 64 + slot_ref[...]
    w = w_ref[...]
    c0, c1, part = row_codes(out_ref.shape[1], 10 * lax.axis_index("c"))

    def weights(c):
        t = jnp.where(c == code[0:1, :], w[0:1, :], 0.0)
        for k in range(1, code.shape[0]):
            t = t + jnp.where(c == code[k : k + 1, :], w[k : k + 1, :], 0.0)
        return t

    tail = weights(c1)
    sets = [weights(c0)] + [jnp.where(part == p, tail, 0.0) for p in range(4)]
    for k, m in enumerate(sets):
        m = jnp.transpose(m)
        hi = m.astype(BF)
        n = m.shape[0]
        out_ref[2 * k * n : (2 * k + 1) * n, :] = hi
        out_ref[(2 * k + 1) * n : (2 * k + 2) * n, :] = (m - hi.astype(F32)).astype(BF)


def combine_body(r_ref, m_ref, own_ref, send_ref):
    n = own_ref.shape[0]
    head = jnp.dot(m_ref[0 : 2 * n, :], r_ref[:, 0:512], preferred_element_type=F32)
    head = head[0:n] + head[n:]
    tail = jnp.dot(m_ref[2 * n :, :], r_ref[:, 512:640], preferred_element_type=F32)
    for k, ref in ((0, own_ref), (1, send_ref)):
        for g in range(2):
            p = 2 * k + g
            s = tail[2 * p * n : (2 * p + 1) * n] + tail[(2 * p + 1) * n : (2 * p + 2) * n]
            ref[:, g * 128 : (g + 1) * 128] = head[:, p * 128 : (p + 1) * 128] + s


def finish_body(own_ref, sent_ref, res_ref, out_ref):
    other = part_of(sent_ref, 1 - lax.axis_index("c"), own_ref.shape[0])
    out_ref[...] = (res_ref[...].astype(F32) + own_ref[...] + other).astype(BF)


def swap(x):
    return lax.ppermute(x, "c", [(0, 1), (1, 0)])


def share(x):
    return lax.all_gather(x, "c", axis=0, tiled=True)


def spread(x, axes):
    return lax.all_to_all(x, axes, split_axis=0, concat_axis=0, tiled=True)


def shards(tokens_in, residual, w_gate, w_up, w_down, expert_ids, slot_pos, route_weights):
    ids, slots, weights = expert_ids.T, slot_pos.T, route_weights.T
    hidden_units = w_gate.shape[2]
    sds = jax.ShapeDtypeStruct
    experts = lax.axis_size(E)
    rows = experts * 10
    chunks = sds((experts * 8, 640), BF)
    gate, up, down = w_gate[0], w_up[0], w_down[0]

    tokens = share(tokens_in)
    outgoing = call(
        dispatch_body, chunks, tokens, ids, slots,
        scratch=[
            pltpu.VMEM(tokens.shape, BF),
            pltpu.VMEM(ids.shape, jnp.int32),
            pltpu.VMEM(ids.shape, jnp.int32),
            pltpu.SemaphoreType.DMA((3,)),
        ],
        stay=True,
        name="dispatch",
    )
    mixing = call(
        weigh_body, sds((10 * ids.shape[1], experts * 8), BF), ids, slots, weights, name="weigh"
    )
    gate_b, up_b, down_b = swap(gate), swap(up), swap(down)
    stacked = call(
        stack_body, sds((2 * gate.shape[0], 2 * hidden_units), BF),
        gate, gate_b, up, up_b, down_b, mixing,
        name="stack",
    )
    arrived = spread(outgoing, LINE)
    partial = call(
        up_body,
        sds((rows, 2 * hidden_units), BF),
        arrived, stacked,
        scratch=[pltpu.VMEM((rows, 512), BF), pltpu.VMEM((experts * 8, 128), F32)],
        name="gate_up",
    )
    parts = spread(partial, R)
    hidden = call(act_body, sds((rows, hidden_units), BF), parts, name="act")
    hidden = spread(hidden, R)
    result = call(
        down_body, chunks, hidden, down, down_b,
        scratch=[pltpu.VMEM((experts * 8, 128), F32)],
        name="down",
    )
    returned = spread(result, LINE)
    half_out = sds(tokens_in.shape, F32)
    own, send = call(combine_body, (half_out, half_out), returned, mixing, name="combine")
    return call(
        finish_body, sds(tokens_in.shape, BF), own, share(send), residual, name="finish"
    )


def solution(mesh):
    fine = Mesh(mesh.devices.reshape(4, 2, 2, 16, 2), T + E)
    in_specs = (
        P(E, T),
        P(E, T),
        P(E, T, None),
        P(E, T, None),
        P(E, None, T),
        P(E, None),
        P(E, None),
        P(E, None),
    )
    return jax.shard_map(
        shards, mesh=fine, in_specs=in_specs, out_specs=P(E, T), check_vma=False
    )
```

time: 135 us -> 134 us (level)
  blocking collectives: 81.4 us -> 90.5 us
  starting transfers between devices: 26.5 us -> 17.6 us
  waiting for transfers between devices: 18.1 us -> 10.6 us
  local copies, waits for them, and re-layouts: 2.07 us -> 5.23 us
  Pallas kernels: 6.47 us -> 8.97 us
    all_gather x1 -> x2, blocking collectives: 4.26 us -> 17.4 us  [share(): return lax.all_gather(x, 'c', axis=0, tiled=True)]
    all_to_all x1, starting transfers between devices: 17.1 us -> 10.9 us  [spread(): return lax.all_to_all(x, axes, split_axis=0, concat_axis=0, tiled=True)]
    all_to_all x1, waiting for transfers between devices: 16 us -> 10.6 us  [spread(): return lax.all_to_all(x, axes, split_axis=0, concat_axis=0, tiled=True)]
    unnamed x12 -> x18, local copies, waits for them, and re-layouts: 0.03 us -> 5.23 us
    all_to_all x3, blocking collectives: 77.1 us -> 73.1 us  [spread(): return lax.all_to_all(x, axes, split_axis=0, concat_axis=0, tiled=True)]
    ppermute x3, starting transfers between devices: 9.38 us -> 6.68 us  [swap(): return lax.ppermute(x, 'c', [(0, 1), (1, 0)])]
    pallas_call x6 -> x8, Pallas kernels: 6.47 us -> 8.97 us  [call(): pl.pallas_call(body, out_shape=out, in_specs=[HBM if stay else VMEM] * le...]
    ppermute x3, waiting for transfers between devices: 2.09 us -> 0.01 us  [swap(): return lax.ppermute(x, 'c', [(0, 1), (1, 0)])]
  transfers between devices with their start and end apart: 4 -> 4, of which waited for: 2 -> 1; matrix products, arithmetic and copies ran while one was open for 2% -> 0% of each run, Pallas kernels for 0% -> 0%
where the time goes in v4:
time: 134 us; the launch traced here: 133 us
  blocking collectives  90.5 us (68%)
  starting transfers between devices  17.6 us (13%)
  waiting for transfers between devices  10.6 us (8%)
  Pallas kernels  8.97 us (7%)
  local copies, waits for them, and re-layouts  5.23 us (4%)
    all_to_all x3, blocking collectives, spread(): return lax.all_to_all(x, axes, split_axis=0, concat_axis=0, tiled=True)  73.1 us
    all_gather x2, blocking collectives, share(): return lax.all_gather(x, 'c', axis=0, tiled=True)  17.4 us
    all_to_all x1, starting transfers between devices, spread(): return lax.all_to_all(x, axes, split_axis=0, concat_axis=0, tiled=True)  10.9 us
    all_to_all x1, waiting for transfers between devices, spread(): return lax.all_to_all(x, axes, split_axis=0, concat_axis=0, tiled=True)  10.6 us
    pallas_call x8, Pallas kernels, call(): pl.pallas_call(body, out_shape=out, in_specs=[HBM if stay else VMEM] * le...  8.97 us
    ppermute x3, starting transfers between devices, swap(): return lax.ppermute(x, 'c', [(0, 1), (1, 0)])  6.68 us
    unnamed x18, local copies, waits for them, and re-layouts  5.23 us
  transfers between devices with their start and end apart: 4, of which 1 were waited for; matrix products, arithmetic and copies ran while one was open for 0% of the time, Pallas kernels for 0%

profile of v4, /device:TPU:1, one launch (start us, length us, event | category | flops | bytes accessed | tf_op | source)
XLA Modules:
  0.0 133.0 jit_solution(7194695954913112520)
XLA Ops:
  0.0 9.9 %all_gather.6.x_hbm = bf16[128,256]{1,0:T(8,128)(2,1)} all-gather(bf16[64,256]{1,0:T(8,128)(2,1)} %param.8), channel_id=1, replica_groups=mesh['y'=4,'xh'=2,'c'=2,'z'=16,'xl'=2] {'c'}, dimensions={0}, use_global_device_ids=true | all-gather | bytes 98304 | tf_op jit(solution)/shard_map/all_gather | solution.py:168
  9.9 2.0 %dispatch.1 = bf16[256,640]{1,0:T(8,128)(2,1)} custom-call(bf16[128,256]{1,0:T(8,128)(2,1)} %all_gather.6.x_hbm, s32[8,64]{1,0:T(8,128)} %bitcast.26, s32[8,64]{1,0:T(8,128)} %bitcast.28), custom_call_target="tpu_custom_call" | custom-call | tf_op jit(solution)/shard_map/dispatch/pallas_call | solution.py:19
  11.9 10.9 %all-to-all-start = ((bf16[32,8,640]{2,1,0:T(8,128)(2,1)}), bf16[32,8,640]{2,1,0:T(8,128)(2,1)}, u32[]{:S(2)}, u32[]{:S(2)}) async-start(bf16[32,8,640]{2,1,0:T(8,128)(2,1)} %bitcast.31), calls=%async_computation | async-start | bytes 655360 | tf_op jit(solution)/shard_map/all_to_all | solution.py:172
  22.8 2.4 %collective-permute-start = (bf16[256,1536]{1,0:T(8,128)(2,1)}, bf16[256,1536]{1,0:T(8,128)(2,1)S(1)}, u32[]{:S(2)}, u32[]{:S(2)}) collective-permute-start(bf16[256,1536]{1,0:T(8,128)(2,1)} %bitcast.20), channel_id=1, source_target_pairs={{0,32},{32,0},{1,33},{33,1},{2,34},{34,2},{3,35},{35,3},{4,36},{36... | collective-permute-start | bytes 2359304 | tf_op jit(solution)/shard_map/ppermute | solution.py:164
  25.2 2.0 %collective-permute-start.1 = (bf16[256,1536]{1,0:T(8,128)(2,1)}, bf16[256,1536]{1,0:T(8,128)(2,1)S(1)}, u32[]{:S(2)}, u32[]{:S(2)}) collective-permute-start(bf16[256,1536]{1,0:T(8,128)(2,1)} %bitcast.22), channel_id=1, source_target_pairs={{0,32},{32,0},{1,33},{33,1},{2,34},{34,2},{3,35},{35,3},{4,36},{36... | collective-permute-start | bytes 2359304 | tf_op jit(solution)/shard_map/ppermute | solution.py:164
  27.2 2.4 %collective-permute-start.2 = (bf16[1536,256]{1,0:T(8,128)(2,1)}, bf16[1536,256]{1,0:T(8,128)(2,1)S(1)}, u32[]{:S(2)}, u32[]{:S(2)}) collective-permute-start(bf16[1536,256]{1,0:T(8,128)(2,1)} %bitcast.24), channel_id=1, source_target_pairs={{0,32},{32,0},{1,33},{33,1},{2,34},{34,2},{3,35},{35,3},{4,36},{36... | collective-permute-start | bytes 2359304 | tf_op jit(solution)/shard_map/ppermute | solution.py:164
  29.5 0.0 copy-start.6
  29.6 0.7 copy-done.6
  30.2 0.0 copy-start.7
  30.2 0.7 copy-done.7
  30.9 0.0 copy-start.8
  30.9 0.7 copy-done.8
  31.6 0.4 weigh.1.__.m_ref
  32.1 0.0 collective-permute-done.gb_ref
  32.1 0.0 collective-permute-done.1.ub_ref
  32.1 0.0 collective-permute-done.2._.v_ref
  32.1 0.0 copy-start.2
  32.1 1.1 copy-done.2
  33.2 0.0 copy-start.3
  33.2 1.1 copy-done.3
  34.4 0.2 stack.1.w_ref
  34.6 0.0 copy-start
  34.6 0.9 copy-done
  35.5 10.6 %all-to-all-done = bf16[32,8,640]{2,1,0:T(8,128)(2,1)} async-done(((bf16[32,8,640]{2,1,0:T(8,128)(2,1)}), bf16[32,8,640]{2,1,0:T(8,128)(2,1)}, u32[]{:S(2)}, u32[]{:S(2)}) %all-to-all-start) | async-done | bytes 327712 | tf_op jit(solution)/shard_map/all_to_all | solution.py:172
  46.1 4.3 %gate_up.1 = bf16[320,3072]{1,0:T(8,128)(2,1)S(1)} custom-call(bf16[256,640]{1,0:T(8,128)(2,1)} %bitcast.3.a_ref, bf16[512,3072]{1,0:T(8,128)(2,1)S(1)} %stack.1.w_ref), custom_call_target="tpu_custom_call" | custom-call | tf_op jit(solution)/shard_map/gate_up/pallas_call | solution.py:19
  50.4 31.4 %all_to_all.44 = bf16[8,40,3072]{2,1,0:T(8,128)(2,1)S(1)} all-to-all(bf16[8,40,3072]{2,1,0:T(8,128)(2,1)S(1)} %bitcast.14), channel_id=1, replica_groups=mesh['y'=4,'xh'=2,'c'=2,'z'=16,'xl'=2] {'y','xh'}, dimensions={0} | all-to-all | bytes 3932160 | tf_op jit(solution)/shard_map/all_to_all | solution.py:172
  81.8 0.0 copy-start.1
  81.8 0.0 copy-start.4
  81.8 0.4 act.1
  82.2 16.0 %all_to_all.45 = bf16[8,40,1536]{2,1,0:T(8,128)(2,1)S(1)} all-to-all(bf16[8,40,1536]{2,1,0:T(8,128)(2,1)S(1)} %bitcast.17), channel_id=1, replica_groups=mesh['y'=4,'xh'=2,'c'=2,'z'=16,'xl'=2] {'y','xh'}, dimensions={0} | all-to-all | bytes 1966080 | tf_op jit(solution)/shard_map/all_to_all | solution.py:172
  98.2 0.0 copy-done.1
  98.2 0.0 copy-done.4
  98.2 0.0 copy-start.5
  98.2 0.7 down.1
  98.9 25.8 %all_to_all.46 = bf16[32,8,640]{2,1,0:T(8,128)(2,1)S(1)} all-to-all(bf16[32,8,640]{2,1,0:T(8,128)(2,1)S(1)} %bitcast.19), channel_id=1, replica_groups=mesh['y'=4,'xh'=2,'c'=2,'z'=16,'xl'=2] {'xl','z'}, dimensions={0} | all-to-all | bytes 655360 | tf_op jit(solution)/shard_map/all_to_all | solution.py:172
  124.7 0.3 combine.1
  124.9 7.4 %all_gather.7.sent_ref = f32[128,256]{1,0:T(8,128)S(1)} all-gather(f32[64,256]{1,0:T(8,128)S(1)} %get-tuple-element.8), channel_id=1, replica_groups=mesh['y'=4,'xh'=2,'c'=2,'z'=16,'xl'=2] {'c'}, dimensions={0}, use_global_device_ids=true | all-gather | bytes 196608 | tf_op jit(solution)/shard_map/all_gather | solution.py:168
  132.4 0.0 copy-done.5
  132.4 0.6 finish.1
Async XLA Ops:
  11.9 34.1 %all-to-all-start = ((bf16[32,8,640]{2,1,0:T(8,128)(2,1)}), bf16[32,8,640]{2,1,0:T(8,128)(2,1)}, u32[]{:S(2)}, u32[]{:S(2)}) async-start(bf16[32,8,640]{2,1,0:T(8,128)(2,1)} %bitcast.31), calls=%async_computation | async-start | bytes 655360 | tf_op jit(solution)/shard_map/all_to_all | solution.py:172
  22.8 9.2 %collective-permute-start = (bf16[256,1536]{1,0:T(8,128)(2,1)}, bf16[256,1536]{1,0:T(8,128)(2,1)S(1)}, u32[]{:S(2)}, u32[]{:S(2)}) collective-permute-start(bf16[256,1536]{1,0:T(8,128)(2,1)} %bitcast.20), channel_id=1, source_target_pairs={{0,32},{32,0},{1,33},{33,1},{2,34},{34,2},{3,35},{35,3},{4,36},{36... | collective-permute-start | bytes 2359304 | tf_op jit(solution)/shard_map/ppermute | solution.py:164
  25.2 6.9 %collective-permute-start.1 = (bf16[256,1536]{1,0:T(8,128)(2,1)}, bf16[256,1536]{1,0:T(8,128)(2,1)S(1)}, u32[]{:S(2)}, u32[]{:S(2)}) collective-permute-start(bf16[256,1536]{1,0:T(8,128)(2,1)} %bitcast.22), channel_id=1, source_target_pairs={{0,32},{32,0},{1,33},{33,1},{2,34},{34,2},{3,35},{35,3},{4,36},{36... | collective-permute-start | bytes 2359304 | tf_op jit(solution)/shard_map/ppermute | solution.py:164
  27.2 4.9 %collective-permute-start.2 = (bf16[1536,256]{1,0:T(8,128)(2,1)}, bf16[1536,256]{1,0:T(8,128)(2,1)S(1)}, u32[]{:S(2)}, u32[]{:S(2)}) collective-permute-start(bf16[1536,256]{1,0:T(8,128)(2,1)} %bitcast.24), channel_id=1, source_target_pairs={{0,32},{32,0},{1,33},{33,1},{2,34},{34,2},{3,35},{35,3},{4,36},{36... | collective-permute-start | bytes 2359304 | tf_op jit(solution)/shard_map/ppermute | solution.py:164
  29.5 0.7 copy-start.6
  30.2 0.7 copy-start.7
  30.9 0.7 copy-start.8
  32.1 1.1 copy-start.2
  33.2 1.1 copy-start.3
  34.6 0.9 copy-start
  81.8 16.4 %copy-start.1 = (bf16[1536,256]{1,0:T(8,128)(2,1)S(1)}, bf16[1536,256]{1,0:T(8,128)(2,1)}, u32[]{:S(2)}) copy-start(bf16[1536,256]{1,0:T(8,128)(2,1)} %copy-done) | copy-start | bytes 2359300
  81.8 16.4 %copy-start.4 = (bf16[1,1536,256]{2,1,0:T(8,128)(2,1)S(1)}, bf16[1,1536,256]{2,1,0:T(8,128)(2,1)}, u32[]{:S(2)}) copy-start(bf16[1,1536,256]{2,1,0:T(8,128)(2,1)} %param.12) | copy-start | bytes 2359300
  98.2 34.2 %copy-start.5 = (bf16[64,256]{1,0:T(8,128)(2,1)S(1)}, bf16[64,256]{1,0:T(8,128)(2,1)}, u32[]{:S(2)}) copy-start(bf16[64,256]{1,0:T(8,128)(2,1)} %res_ref.1) | copy-start | bytes 98308

commit v5 on v4

--- a/solution.py
+++ b/solution.py
@@ -12,17 +12,16 @@
 E = ("z", "xl")
 LINE = ("xl", "z")
 VMEM = pl.BlockSpec(memory_space=pltpu.VMEM)
-HBM = pl.BlockSpec(memory_space=pltpu.HBM)
-
-
-def call(body, out, *args, name, limit=16 << 20, scratch=(), stay=False):
+
+
+def call(body, out, *args, name, limit=16 << 20, scratch=()):
     return pl.pallas_call(
         body,
         out_shape=out,
-        in_specs=[HBM if stay else VMEM] * len(args),
+        in_specs=[VMEM] * len(args),
         out_specs=jax.tree.map(lambda _: VMEM, out),
         scratch_shapes=list(scratch),
-        compiler_params=pltpu.CompilerParams(vmem_limit_bytes=None if stay else limit),
+        compiler_params=pltpu.CompilerParams(vmem_limit_bytes=limit),
         name=name,
     )(*args)
 
@@ -39,19 +38,11 @@
     return ref[pl.ds(pl.multiple_of(index * count, count), count), :]
 
 
-def dispatch_body(x_hbm, ids_hbm, slot_hbm, out_ref, x_ref, ids_ref, slot_ref, sems):
-    copies = [
-        pltpu.make_async_copy(a, b, sems.at[i])
-        for i, (a, b) in enumerate(((ids_hbm, ids_ref), (slot_hbm, slot_ref), (x_hbm, x_ref)))
-    ]
-    for c in copies:
-        c.start()
+def dispatch_body(x_ref, code_ref, out_ref):
     core = lax.axis_index("c")
     n = x_ref.shape[0] // 2
     c0, c1, part = row_codes(out_ref.shape[0], 10 * core)
-    for c in copies:
-        c.wait()
-    code = ids_ref[...] * 64 + slot_ref[...]
+    code = code_ref[...]
     own, other = part_of(x_ref, core, n), part_of(x_ref, 1 - core, n)
 
     def pick(c):
@@ -87,10 +78,7 @@
     for g in range(4):
         x_ref[n:, g * 128 : (g + 1) * 128] = t_ref[pl.ds(g, n // 4, stride=4), :].astype(BF)
 
-    @pl.loop(0, out_ref.shape[0] // 64)
-    def _(i):
-        s = pl.ds(pl.multiple_of(i * 64, 64), 64)
-        out_ref[s, :] = jnp.dot(x_ref[s, :], w_ref[...], preferred_element_type=F32).astype(BF)
+    out_ref[...] = jnp.dot(x_ref[...], w_ref[...], preferred_element_type=F32).astype(BF)
 
 
 def act_body(p_ref, h_ref):
@@ -122,10 +110,10 @@
     out_ref[:, 512:640] = t_ref[...].astype(BF)
 
 
-def weigh_body(ids_ref, slot_ref, w_ref, out_ref):
-    code = ids_ref[...] * 64 + slot_ref[...]
+def weigh_body(code_ref, w_ref, out_ref):
+    code = code_ref[...]
     w = w_ref[...]
-    c0, c1, part = row_codes(out_ref.shape[1], 10 * lax.axis_index("c"))
+    c0, c1, _ = row_codes(out_ref.shape[1], 10 * lax.axis_index("c"))
 
     def weights(c):
         t = jnp.where(c == code[0:1, :], w[0:1, :], 0.0)
@@ -133,9 +121,7 @@
             t = t + jnp.where(c == code[k : k + 1, :], w[k : k + 1, :], 0.0)
         return t
 
-    tail = weights(c1)
-    sets = [weights(c0)] + [jnp.where(part == p, tail, 0.0) for p in range(4)]
-    for k, m in enumerate(sets):
+    for k, m in enumerate((weights(c0), weights(c1))):
         m = jnp.transpose(m)
         hi = m.astype(BF)
         n = m.shape[0]
@@ -147,12 +133,15 @@
     n = own_ref.shape[0]
     head = jnp.dot(m_ref[0 : 2 * n, :], r_ref[:, 0:512], preferred_element_type=F32)
     head = head[0:n] + head[n:]
-    tail = jnp.dot(m_ref[2 * n :, :], r_ref[:, 512:640], preferred_element_type=F32)
+    rest = r_ref[:, 512:640]
+    part = lax.rem(lax.broadcasted_iota(jnp.int32, rest.shape, 0), 4)
+    parts = [jnp.where(part == p, rest, 0.0).astype(BF) for p in range(4)]
+    tail = jnp.dot(m_ref[2 * n :, :], jnp.concatenate(parts, axis=1), preferred_element_type=F32)
     for k, ref in ((0, own_ref), (1, send_ref)):
         for g in range(2):
             p = 2 * k + g
-            s = tail[2 * p * n : (2 * p + 1) * n] + tail[(2 * p + 1) * n : (2 * p + 2) * n]
-            ref[:, g * 128 : (g + 1) * 128] = head[:, p * 128 : (p + 1) * 128] + s
+            s = slice(p * 128, (p + 1) * 128)
+            ref[:, g * 128 : (g + 1) * 128] = head[:, s] + tail[0:n, s] + tail[n:, s]
 
 
 def finish_body(own_ref, sent_ref, res_ref, out_ref):
@@ -173,7 +162,7 @@
 
 
 def shards(tokens_in, residual, w_gate, w_up, w_down, expert_ids, slot_pos, route_weights):
-    ids, slots, weights = expert_ids.T, slot_pos.T, route_weights.T
+    code, weights = (expert_ids * 64 + slot_pos).T, route_weights.T
     hidden_units = w_gate.shape[2]
     sds = jax.ShapeDtypeStruct
     experts = lax.axis_size(E)
@@ -182,19 +171,9 @@
     gate, up, down = w_gate[0], w_up[0], w_down[0]
 
     tokens = share(tokens_in)
-    outgoing = call(
-        dispatch_body, chunks, tokens, ids, slots,
-        scratch=[
-            pltpu.VMEM(tokens.shape, BF),
-            pltpu.VMEM(ids.shape, jnp.int32),
-            pltpu.VMEM(ids.shape, jnp.int32),
-            pltpu.SemaphoreType.DMA((3,)),
-        ],
-        stay=True,
-        name="dispatch",
-    )
+    outgoing = call(dispatch_body, chunks, tokens, code, name="dispatch")
     mixing = call(
-        weigh_body, sds((10 * ids.shape[1], experts * 8), BF), ids, slots, weights, name="weigh"
+        weigh_body, sds((4 * code.shape[1], experts * 8), BF), code, weights, name="weigh"
     )
     gate_b, up_b, down_b = swap(gate), swap(up), swap(down)
     stacked = call(

time: 134 us -> 129 us (0.963)
  Pallas kernels: 8.97 us -> 4.86 us
    pallas_call x8, Pallas kernels: 8.97 us -> 4.86 us  [call(): pl.pallas_call(body, out_shape=out, in_specs=[VMEM] * len(args), out_spec...]
  transfers between devices with their start and end apart: 4 -> 4, of which waited for: 1 -> 2; matrix products, arithmetic and copies ran while one was open for 0% -> 0% of each run, Pallas kernels for 0% -> 0%
where the time goes in v5:
time: 129 us; the launch traced here: 128 us
  blocking collectives  89.2 us (69%)
  starting transfers between devices  17.6 us (14%)
  waiting for transfers between devices  11.3 us (9%)
  Pallas kernels  4.86 us (4%)
  local copies, waits for them, and re-layouts  4.53 us (4%)
    all_to_all x3, blocking collectives, spread(): return lax.all_to_all(x, axes, split_axis=0, concat_axis=0, tiled=True)  73.1 us
    all_gather x2, blocking collectives, share(): return lax.all_gather(x, 'c', axis=0, tiled=True)  16 us
    all_to_all x1, starting transfers between devices, spread(): return lax.all_to_all(x, axes, split_axis=0, concat_axis=0, tiled=True)  10.8 us
    all_to_all x1, waiting for transfers between devices, spread(): return lax.all_to_all(x, axes, split_axis=0, concat_axis=0, tiled=True)  10.2 us
    ppermute x3, starting transfers between devices, swap(): return lax.ppermute(x, 'c', [(0, 1), (1, 0)])  6.87 us
    pallas_call x8, Pallas kernels, call(): pl.pallas_call(body, out_shape=out, in_specs=[VMEM] * len(args), out_spec...  4.86 us
    unnamed x18, local copies, waits for them, and re-layouts  4.53 us
  transfers between devices with their start and end apart: 4, of which 2 were waited for; matrix products, arithmetic and copies ran while one was open for 0% of the time, Pallas kernels for 0%

profile of v5, /device:TPU:1, one launch (start us, length us, event | category | flops | bytes accessed | tf_op | source)
XLA Modules:
  0.0 128.3 jit_solution(895403455785927563)
XLA Ops:
  0.0 8.6 %all_gather.6.x_ref = bf16[128,256]{1,0:T(8,128)(2,1)S(1)} all-gather(bf16[64,256]{1,0:T(8,128)(2,1)} %param.8), channel_id=1, replica_groups=mesh['y'=4,'xh'=2,'c'=2,'z'=16,'xl'=2] {'c'}, dimensions={0}, use_global_device_ids=true | all-gather | bytes 98304 | tf_op jit(solution)/shard_map/all_gather | solution.py:157
  8.6 0.7 add_bitcast_fusion.code_ref
  9.3 1.1 dispatch.1
  10.4 10.8 %all-to-all-start = ((bf16[32,8,640]{2,1,0:T(8,128)(2,1)}), bf16[32,8,640]{2,1,0:T(8,128)(2,1)S(1)}, u32[]{:S(2)}, u32[]{:S(2)}) async-start(bf16[32,8,640]{2,1,0:T(8,128)(2,1)} %bitcast.1), calls=%async_computation | async-start | bytes 655360 | tf_op jit(solution)/shard_map/all_to_all | solution.py:161
  21.2 2.5 %collective-permute-start = (bf16[256,1536]{1,0:T(8,128)(2,1)}, bf16[256,1536]{1,0:T(8,128)(2,1)S(1)}, u32[]{:S(2)}, u32[]{:S(2)}) collective-permute-start(bf16[256,1536]{1,0:T(8,128)(2,1)} %bitcast.21), channel_id=1, source_target_pairs={{0,32},{32,0},{1,33},{33,1},{2,34},{34,2},{3,35},{35,3},{4,36},{36... | collective-permute-start | bytes 2359304 | tf_op jit(solution)/shard_map/ppermute | solution.py:153
  23.7 1.9 %collective-permute-start.1 = (bf16[256,1536]{1,0:T(8,128)(2,1)}, bf16[256,1536]{1,0:T(8,128)(2,1)S(1)}, u32[]{:S(2)}, u32[]{:S(2)}) collective-permute-start(bf16[256,1536]{1,0:T(8,128)(2,1)} %bitcast.23), channel_id=1, source_target_pairs={{0,32},{32,0},{1,33},{33,1},{2,34},{34,2},{3,35},{35,3},{4,36},{36... | collective-permute-start | bytes 2359304 | tf_op jit(solution)/shard_map/ppermute | solution.py:153
  25.7 2.4 %collective-permute-start.2 = (bf16[1536,256]{1,0:T(8,128)(2,1)}, bf16[1536,256]{1,0:T(8,128)(2,1)S(1)}, u32[]{:S(2)}, u32[]{:S(2)}) collective-permute-start(bf16[1536,256]{1,0:T(8,128)(2,1)} %bitcast.25), channel_id=1, source_target_pairs={{0,32},{32,0},{1,33},{33,1},{2,34},{34,2},{3,35},{35,3},{4,36},{36... | collective-permute-start | bytes 2359304 | tf_op jit(solution)/shard_map/ppermute | solution.py:153
  28.1 0.0 copy-start.8
  28.1 0.7 copy-done.8
  28.8 0.3 weigh.1.__.m_ref
  29.1 0.0 collective-permute-done.gb_ref
  29.1 0.0 collective-permute-done.1.ub_ref
  29.1 1.0 collective-permute-done.2._.v_ref
  30.2 0.0 copy-start.4
  30.2 1.1 copy-done.4
  31.3 0.0 copy-start.5
  31.3 1.1 copy-done.5
  32.4 0.2 stack.1.w_ref
  32.7 0.0 copy-start
  32.7 0.9 copy-done
  33.6 0.0 copy-start.2
  33.6 0.7 copy-done.2
  34.2 10.2 %all-to-all-done = bf16[32,8,640]{2,1,0:T(8,128)(2,1)S(1)} async-done(((bf16[32,8,640]{2,1,0:T(8,128)(2,1)}), bf16[32,8,640]{2,1,0:T(8,128)(2,1)S(1)}, u32[]{:S(2)}, u32[]{:S(2)}) %all-to-all-start) | async-done | bytes 327712 | tf_op jit(solution)/shard_map/all_to_all | solution.py:161
  44.4 1.2 gate_up.1
  45.6 31.0 %all_to_all.44 = bf16[8,40,3072]{2,1,0:T(8,128)(2,1)S(1)} all-to-all(bf16[8,40,3072]{2,1,0:T(8,128)(2,1)S(1)} %bitcast.14), channel_id=1, replica_groups=mesh['y'=4,'xh'=2,'c'=2,'z'=16,'xl'=2] {'y','xh'}, dimensions={0} | all-to-all | bytes 3932160 | tf_op jit(solution)/shard_map/all_to_all | solution.py:161
  76.6 0.0 copy-start.1
  76.6 0.0 copy-start.6
  76.6 0.4 act.1
  77.0 16.4 %all_to_all.45 = bf16[8,40,1536]{2,1,0:T(8,128)(2,1)S(1)} all-to-all(bf16[8,40,1536]{2,1,0:T(8,128)(2,1)S(1)} %bitcast.17), channel_id=1, replica_groups=mesh['y'=4,'xh'=2,'c'=2,'z'=16,'xl'=2] {'y','xh'}, dimensions={0} | all-to-all | bytes 1966080 | tf_op jit(solution)/shard_map/all_to_all | solution.py:161
  93.4 0.0 copy-start.3
  93.4 0.0 copy-done.1
  93.4 0.0 copy-done.6
  93.4 0.0 copy-start.7
  93.4 0.7 down.1
  94.1 25.8 %all_to_all.46 = bf16[32,8,640]{2,1,0:T(8,128)(2,1)S(1)} all-to-all(bf16[32,8,640]{2,1,0:T(8,128)(2,1)S(1)} %bitcast.20), channel_id=1, replica_groups=mesh['y'=4,'xh'=2,'c'=2,'z'=16,'xl'=2] {'xl','z'}, dimensions={0} | all-to-all | bytes 655360 | tf_op jit(solution)/shard_map/all_to_all | solution.py:161
  119.9 0.0 copy-done.3
  119.9 0.3 combine.1
  120.2 7.4 %all_gather.7.sent_ref = f32[128,256]{1,0:T(8,128)S(1)} all-gather(f32[64,256]{1,0:T(8,128)S(1)} %get-tuple-element.8), channel_id=1, replica_groups=mesh['y'=4,'xh'=2,'c'=2,'z'=16,'xl'=2] {'c'}, dimensions={0}, use_global_device_ids=true | all-gather | bytes 196608 | tf_op jit(solution)/shard_map/all_gather | solution.py:157
  127.6 0.0 copy-done.7
  127.6 0.6 finish.1
Async XLA Ops:
  10.4 34.0 %all-to-all-start = ((bf16[32,8,640]{2,1,0:T(8,128)(2,1)}), bf16[32,8,640]{2,1,0:T(8,128)(2,1)S(1)}, u32[]{:S(2)}, u32[]{:S(2)}) async-start(bf16[32,8,640]{2,1,0:T(8,128)(2,1)} %bitcast.1), calls=%async_computation | async-start | bytes 655360 | tf_op jit(solution)/shard_map/all_to_all | solution.py:161
  21.2 7.9 %collective-permute-start = (bf16[256,1536]{1,0:T(8,128)(2,1)}, bf16[256,1536]{1,0:T(8,128)(2,1)S(1)}, u32[]{:S(2)}, u32[]{:S(2)}) collective-permute-start(bf16[256,1536]{1,0:T(8,128)(2,1)} %bitcast.21), channel_id=1, source_target_pairs={{0,32},{32,0},{1,33},{33,1},{2,34},{34,2},{3,35},{35,3},{4,36},{36... | collective-permute-start | bytes 2359304 | tf_op jit(solution)/shard_map/ppermute | solution.py:153
  23.7 5.4 %collective-permute-start.1 = (bf16[256,1536]{1,0:T(8,128)(2,1)}, bf16[256,1536]{1,0:T(8,128)(2,1)S(1)}, u32[]{:S(2)}, u32[]{:S(2)}) collective-permute-start(bf16[256,1536]{1,0:T(8,128)(2,1)} %bitcast.23), channel_id=1, source_target_pairs={{0,32},{32,0},{1,33},{33,1},{2,34},{34,2},{3,35},{35,3},{4,36},{36... | collective-permute-start | bytes 2359304 | tf_op jit(solution)/shard_map/ppermute | solution.py:153
  25.7 4.5 %collective-permute-start.2 = (bf16[1536,256]{1,0:T(8,128)(2,1)}, bf16[1536,256]{1,0:T(8,128)(2,1)S(1)}, u32[]{:S(2)}, u32[]{:S(2)}) collective-permute-start(bf16[1536,256]{1,0:T(8,128)(2,1)} %bitcast.25), channel_id=1, source_target_pairs={{0,32},{32,0},{1,33},{33,1},{2,34},{34,2},{3,35},{35,3},{4,36},{36... | collective-permute-start | bytes 2359304 | tf_op jit(solution)/shard_map/ppermute | solution.py:153
  28.1 0.7 copy-start.8
  30.2 1.1 copy-start.4
  31.3 1.1 copy-start.5
  32.7 0.9 copy-start
  33.6 0.7 copy-start.2
  76.6 16.8 %copy-start.1 = (bf16[1536,256]{1,0:T(8,128)(2,1)S(1)}, bf16[1536,256]{1,0:T(8,128)(2,1)}, u32[]{:S(2)}) copy-start(bf16[1536,256]{1,0:T(8,128)(2,1)} %copy-done) | copy-start | bytes 2359300
  76.6 16.8 %copy-start.6 = (bf16[1,1536,256]{2,1,0:T(8,128)(2,1)S(1)}, bf16[1,1536,256]{2,1,0:T(8,128)(2,1)}, u32[]{:S(2)}) copy-start(bf16[1,1536,256]{2,1,0:T(8,128)(2,1)} %param.12) | copy-start | bytes 2359300
  93.4 26.5 %copy-start.3 = (bf16[256,256]{1,0:T(8,128)(2,1)S(1)}, bf16[256,256]{1,0:T(8,128)(2,1)}, u32[]{:S(2)}) copy-start(bf16[256,256]{1,0:T(8,128)(2,1)} %copy-done.2) | copy-start | bytes 393220
  93.4 34.2 %copy-start.7 = (bf16[64,256]{1,0:T(8,128)(2,1)S(1)}, bf16[64,256]{1,0:T(8,128)(2,1)}, u32[]{:S(2)}) copy-start(bf16[64,256]{1,0:T(8,128)(2,1)} %res_ref.1) | copy-start | bytes 98308

commit v6 on v5

--- a/solution.py
+++ b/solution.py
@@ -9,8 +9,8 @@
 F32 = jnp.float32
 T = ("y", "xh", "c")
 R = ("y", "xh")
-E = ("z", "xl")
-LINE = ("xl", "z")
+E = ("za", "zb", "xl")
+LINE = ("xl", "zb", "za")
 VMEM = pl.BlockSpec(memory_space=pltpu.VMEM)
 
 
@@ -26,11 +26,20 @@
     )(*args)
 
 
+def expert_of(chunk):
+    total, left = 0, chunk
+    for axis in reversed(LINE):
+        size = lax.axis_size(axis)
+        stride = lax.axis_size(E[E.index(axis) + 1 :]) if axis != E[-1] else 1
+        total = total + lax.rem(left, size) * stride
+        left = left // size
+    return total
+
+
 def row_codes(rows, first):
     r = lax.broadcasted_iota(jnp.int32, (rows, 1), 0)
     d, j = r // 8, lax.rem(r, 8)
-    experts = rows // 8
-    base = (lax.rem(d, experts // 2) * 2 + d // (experts // 2)) * 64 + first
+    base = expert_of(d) * 64 + first
     return base + j, base + 8 + j // 4, lax.rem(j, 4)
 
 
@@ -206,7 +215,7 @@
 
 
 def solution(mesh):
-    fine = Mesh(mesh.devices.reshape(4, 2, 2, 16, 2), T + E)
+    fine = Mesh(mesh.devices.reshape(4, 2, 2, 4, 4, 2), T + E)
     in_specs = (
         P(E, T),
         P(E, T),

time: 129 us -> 126 us (0.977); the launches traced: 128 us -> 124 us
  waiting for transfers between devices: 11.3 us -> 2.98 us
  blocking collectives: 89.2 us -> 93 us
    all_to_all x1, waiting for transfers between devices: 10.2 us -> 1.97 us  [spread(): return lax.all_to_all(x, axes, split_axis=0, concat_axis=0, tiled=True)]
    all_to_all x3, blocking collectives: 73.1 us -> 75.2 us  [spread(): return lax.all_to_all(x, axes, split_axis=0, concat_axis=0, tiled=True)]
    all_gather x2, blocking collectives: 16 us -> 17.8 us  [share(): return lax.all_gather(x, 'c', axis=0, tiled=True)]
where the time goes in v6:
time: 126 us; the launch traced here: 124 us
  blocking collectives  93 us (74%)
  starting transfers between devices  17.6 us (14%)
  Pallas kernels  4.92 us (4%)
  local copies, waits for them, and re-layouts  4.53 us (4%)
  waiting for transfers between devices  2.98 us (2%)
    all_to_all x3, blocking collectives, spread(): return lax.all_to_all(x, axes, split_axis=0, concat_axis=0, tiled=True)  75.2 us
    all_gather x2, blocking collectives, share(): return lax.all_gather(x, 'c', axis=0, tiled=True)  17.8 us
    all_to_all x1, starting transfers between devices, spread(): return lax.all_to_all(x, axes, split_axis=0, concat_axis=0, tiled=True)  10.8 us
    ppermute x3, starting transfers between devices, swap(): return lax.ppermute(x, 'c', [(0, 1), (1, 0)])  6.87 us
    pallas_call x8, Pallas kernels, call(): pl.pallas_call(body, out_shape=out, in_specs=[VMEM] * len(args), out_spec...  4.92 us
    unnamed x18, local copies, waits for them, and re-layouts  4.53 us
  transfers between devices with their start and end apart: 4, of which 2 were waited for; matrix products, arithmetic and copies ran while one was open for 0% of the time, Pallas kernels for 0%

profile of v6, /device:TPU:1, one launch (start us, length us, event | category | flops | bytes accessed | tf_op | source)
XLA Modules:
  0.0 123.8 jit_solution(337248358343566862)
XLA Ops:
  0.0 8.6 %all_gather.6.x_ref = bf16[128,256]{1,0:T(8,128)(2,1)S(1)} all-gather(bf16[64,256]{1,0:T(8,128)(2,1)} %param.8), channel_id=1, replica_groups=mesh['y'=4,'xh'=2,'c'=2,'za'=4,'zb'=4,'xl'=2] {'c'}, dimensions={0}, use_global_device_ids=true | all-gather | bytes 98304 | tf_op jit(solution)/shard_map/all_gather | solution.py:166
  8.6 0.7 add_bitcast_fusion.code_ref
  9.3 1.1 dispatch.1
  10.4 10.8 %all-to-all-start = ((bf16[32,8,640]{2,1,0:T(8,128)(2,1)}), bf16[32,8,640]{2,1,0:T(8,128)(2,1)S(1)}, u32[]{:S(2)}, u32[]{:S(2)}) async-start(bf16[32,8,640]{2,1,0:T(8,128)(2,1)} %bitcast.1), calls=%async_computation | async-start | bytes 655360 | tf_op jit(solution)/shard_map/all_to_all | solution.py:170
  21.2 2.5 %collective-permute-start = (bf16[256,1536]{1,0:T(8,128)(2,1)}, bf16[256,1536]{1,0:T(8,128)(2,1)S(1)}, u32[]{:S(2)}, u32[]{:S(2)}) collective-permute-start(bf16[256,1536]{1,0:T(8,128)(2,1)} %bitcast.21), channel_id=1, source_target_pairs={{0,32},{32,0},{1,33},{33,1},{2,34},{34,2},{3,35},{35,3},{4,36},{36... | collective-permute-start | bytes 2359304 | tf_op jit(solution)/shard_map/ppermute | solution.py:162
  23.7 1.9 %collective-permute-start.1 = (bf16[256,1536]{1,0:T(8,128)(2,1)}, bf16[256,1536]{1,0:T(8,128)(2,1)S(1)}, u32[]{:S(2)}, u32[]{:S(2)}) collective-permute-start(bf16[256,1536]{1,0:T(8,128)(2,1)} %bitcast.23), channel_id=1, source_target_pairs={{0,32},{32,0},{1,33},{33,1},{2,34},{34,2},{3,35},{35,3},{4,36},{36... | collective-permute-start | bytes 2359304 | tf_op jit(solution)/shard_map/ppermute | solution.py:162
  25.7 2.4 %collective-permute-start.2 = (bf16[1536,256]{1,0:T(8,128)(2,1)}, bf16[1536,256]{1,0:T(8,128)(2,1)S(1)}, u32[]{:S(2)}, u32[]{:S(2)}) collective-permute-start(bf16[1536,256]{1,0:T(8,128)(2,1)} %bitcast.25), channel_id=1, source_target_pairs={{0,32},{32,0},{1,33},{33,1},{2,34},{34,2},{3,35},{35,3},{4,36},{36... | collective-permute-start | bytes 2359304 | tf_op jit(solution)/shard_map/ppermute | solution.py:162
  28.1 0.0 copy-start.8
  28.1 0.7 copy-done.8
  28.8 0.4 weigh.1.__.m_ref
  29.2 0.0 collective-permute-done.gb_ref
  29.2 0.0 collective-permute-done.1.ub_ref
  29.2 1.0 collective-permute-done.2._.v_ref
  30.2 0.0 copy-start.4
  30.2 1.1 copy-done.4
  31.3 0.0 copy-start.5
  31.3 1.1 copy-done.5
  32.5 0.2 stack.1.w_ref
  32.7 0.0 copy-start
  32.7 0.9 copy-done
  33.6 0.0 copy-start.2
  33.6 0.7 copy-done.2
  34.2 2.0 %all-to-all-done = bf16[32,8,640]{2,1,0:T(8,128)(2,1)S(1)} async-done(((bf16[32,8,640]{2,1,0:T(8,128)(2,1)}), bf16[32,8,640]{2,1,0:T(8,128)(2,1)S(1)}, u32[]{:S(2)}, u32[]{:S(2)}) %all-to-all-start) | async-done | bytes 327712 | tf_op jit(solution)/shard_map/all_to_all | solution.py:170
  36.2 1.2 gate_up.1
  37.4 27.4 %all_to_all.44 = bf16[8,40,3072]{2,1,0:T(8,128)(2,1)S(1)} all-to-all(bf16[8,40,3072]{2,1,0:T(8,128)(2,1)S(1)} %bitcast.14), channel_id=1, replica_groups=mesh['y'=4,'xh'=2,'c'=2,'za'=4,'zb'=4,'xl'=2] {'y','xh'}, dimensions={0} | all-to-all | bytes 3932160 | tf_op jit(solution)/shard_map/all_to_all | solution.py:170
  64.8 0.0 copy-start.1
  64.8 0.0 copy-start.6
  64.8 0.4 act.1
  65.2 14.1 %all_to_all.45 = bf16[8,40,1536]{2,1,0:T(8,128)(2,1)S(1)} all-to-all(bf16[8,40,1536]{2,1,0:T(8,128)(2,1)S(1)} %bitcast.17), channel_id=1, replica_groups=mesh['y'=4,'xh'=2,'c'=2,'za'=4,'zb'=4,'xl'=2] {'y','xh'}, dimensions={0} | all-to-all | bytes 1966080 | tf_op jit(solution)/shard_map/all_to_all | solution.py:170
  79.3 0.0 copy-start.3
  79.3 0.0 copy-done.1
  79.3 0.0 copy-done.6
  79.3 0.0 copy-start.7
  79.3 0.7 down.1
  80.0 33.7 %all_to_all.46 = bf16[32,8,640]{2,1,0:T(8,128)(2,1)S(1)} all-to-all(bf16[32,8,640]{2,1,0:T(8,128)(2,1)S(1)} %bitcast.20), channel_id=1, replica_groups=mesh['y'=4,'xh'=2,'c'=2,'za'=4,'zb'=4,'xl'=2] {'xl','zb','za'}, dimensions={0} | all-to-all | bytes 655360 | tf_op jit(solution)/shard_map/all_to_all | solution.py:170
  113.7 0.0 copy-done.3
  113.8 0.3 combine.1
  114.0 9.2 %all_gather.7.sent_ref = f32[128,256]{1,0:T(8,128)S(1)} all-gather(f32[64,256]{1,0:T(8,128)S(1)} %get-tuple-element.8), channel_id=1, replica_groups=mesh['y'=4,'xh'=2,'c'=2,'za'=4,'zb'=4,'xl'=2] {'c'}, dimensions={0}, use_global_device_ids=true | all-gather | bytes 196608 | tf_op jit(solution)/shard_map/all_gather | solution.py:166
  123.2 0.0 copy-done.7
  123.2 0.6 finish.1
Async XLA Ops:
  10.4 25.8 %all-to-all-start = ((bf16[32,8,640]{2,1,0:T(8,128)(2,1)}), bf16[32,8,640]{2,1,0:T(8,128)(2,1)S(1)}, u32[]{:S(2)}, u32[]{:S(2)}) async-start(bf16[32,8,640]{2,1,0:T(8,128)(2,1)} %bitcast.1), calls=%async_computation | async-start | bytes 655360 | tf_op jit(solution)/shard_map/all_to_all | solution.py:170
  21.2 8.0 %collective-permute-start = (bf16[256,1536]{1,0:T(8,128)(2,1)}, bf16[256,1536]{1,0:T(8,128)(2,1)S(1)}, u32[]{:S(2)}, u32[]{:S(2)}) collective-permute-start(bf16[256,1536]{1,0:T(8,128)(2,1)} %bitcast.21), channel_id=1, source_target_pairs={{0,32},{32,0},{1,33},{33,1},{2,34},{34,2},{3,35},{35,3},{4,36},{36... | collective-permute-start | bytes 2359304 | tf_op jit(solution)/shard_map/ppermute | solution.py:162
  23.7 5.4 %collective-permute-start.1 = (bf16[256,1536]{1,0:T(8,128)(2,1)}, bf16[256,1536]{1,0:T(8,128)(2,1)S(1)}, u32[]{:S(2)}, u32[]{:S(2)}) collective-permute-start(bf16[256,1536]{1,0:T(8,128)(2,1)} %bitcast.23), channel_id=1, source_target_pairs={{0,32},{32,0},{1,33},{33,1},{2,34},{34,2},{3,35},{35,3},{4,36},{36... | collective-permute-start | bytes 2359304 | tf_op jit(solution)/shard_map/ppermute | solution.py:162
  25.7 4.5 %collective-permute-start.2 = (bf16[1536,256]{1,0:T(8,128)(2,1)}, bf16[1536,256]{1,0:T(8,128)(2,1)S(1)}, u32[]{:S(2)}, u32[]{:S(2)}) collective-permute-start(bf16[1536,256]{1,0:T(8,128)(2,1)} %bitcast.25), channel_id=1, source_target_pairs={{0,32},{32,0},{1,33},{33,1},{2,34},{34,2},{3,35},{35,3},{4,36},{36... | collective-permute-start | bytes 2359304 | tf_op jit(solution)/shard_map/ppermute | solution.py:162
  28.1 0.7 copy-start.8
  30.2 1.1 copy-start.4
  31.3 1.1 copy-start.5
  32.7 0.9 copy-start
  33.6 0.7 copy-start.2
  64.8 14.5 %copy-start.1 = (bf16[1536,256]{1,0:T(8,128)(2,1)S(1)}, bf16[1536,256]{1,0:T(8,128)(2,1)}, u32[]{:S(2)}) copy-start(bf16[1536,256]{1,0:T(8,128)(2,1)} %copy-done) | copy-start | bytes 2359300
  64.8 14.5 %copy-start.6 = (bf16[1,1536,256]{2,1,0:T(8,128)(2,1)S(1)}, bf16[1,1536,256]{2,1,0:T(8,128)(2,1)}, u32[]{:S(2)}) copy-start(bf16[1,1536,256]{2,1,0:T(8,128)(2,1)} %param.12) | copy-start | bytes 2359300
  79.3 34.4 %copy-start.3 = (bf16[256,256]{1,0:T(8,128)(2,1)S(1)}, bf16[256,256]{1,0:T(8,128)(2,1)}, u32[]{:S(2)}) copy-start(bf16[256,256]{1,0:T(8,128)(2,1)} %copy-done.2) | copy-start | bytes 393220
  79.3 43.9 %copy-start.7 = (bf16[64,256]{1,0:T(8,128)(2,1)S(1)}, bf16[64,256]{1,0:T(8,128)(2,1)}, u32[]{:S(2)}) copy-start(bf16[64,256]{1,0:T(8,128)(2,1)} %res_ref.1) | copy-start | bytes 98308

commit v7 on v6

--- a/solution.py
+++ b/solution.py
@@ -9,8 +9,8 @@
 F32 = jnp.float32
 T = ("y", "xh", "c")
 R = ("y", "xh")
-E = ("za", "zb", "xl")
-LINE = ("xl", "zb", "za")
+E = ("z3", "z2", "z1", "z0", "xl")
+LINE = ("xl", "z0", "z1", "z3", "z2")
 VMEM = pl.BlockSpec(memory_space=pltpu.VMEM)
 
 
@@ -215,7 +215,7 @@
 
 
 def solution(mesh):
-    fine = Mesh(mesh.devices.reshape(4, 2, 2, 4, 4, 2), T + E)
+    fine = Mesh(mesh.devices.reshape(4, 2, 2, 2, 2, 2, 2, 2), T + E)
     in_specs = (
         P(E, T),
         P(E, T),

time: 126 us -> 124 us (0.984); the launches traced: 124 us -> 124 us
  blocking collectives: 93 us -> 91 us
  waiting for transfers between devices: 2.98 us -> 4.59 us
    all_to_all x3, blocking collectives: 75.2 us -> 73.2 us  [spread(): return lax.all_to_all(x, axes, split_axis=0, concat_axis=0, tiled=True)]
    all_to_all x1, waiting for transfers between devices: 1.97 us -> 3.76 us  [spread(): return lax.all_to_all(x, axes, split_axis=0, concat_axis=0, tiled=True)]
  transfers between devices with their start and end apart: 4 -> 4, of which waited for: 2 -> 2; matrix products, arithmetic and copies ran while one was open for 0% -> 0% of each run, Pallas kernels for 0% -> 1%
where the time goes in v7:
time: 124 us
  blocking collectives  91 us (73%)
  starting transfers between devices  17.6 us (14%)
  Pallas kernels  5.25 us (4%)
  waiting for transfers between devices  4.59 us (4%)
  local copies, waits for them, and re-layouts  4.53 us (4%)
    all_to_all x3, blocking collectives, spread(): return lax.all_to_all(x, axes, split_axis=0, concat_axis=0, tiled=True)  73.2 us
    all_gather x2, blocking collectives, share(): return lax.all_gather(x, 'c', axis=0, tiled=True)  17.8 us
    all_to_all x1, starting transfers between devices, spread(): return lax.all_to_all(x, axes, split_axis=0, concat_axis=0, tiled=True)  10.8 us
    ppermute x3, starting transfers between devices, swap(): return lax.ppermute(x, 'c', [(0, 1), (1, 0)])  6.87 us
    pallas_call x8, Pallas kernels, call(): pl.pallas_call(body, out_shape=out, in_specs=[VMEM] * len(args), out_spec...  5.25 us
    unnamed x18, local copies, waits for them, and re-layouts  4.53 us
    all_to_all x1, waiting for transfers between devices, spread(): return lax.all_to_all(x, axes, split_axis=0, concat_axis=0, tiled=True)  3.76 us
  transfers between devices with their start and end apart: 4, of which 2 were waited for; matrix products, arithmetic and copies ran while one was open for 0% of the time, Pallas kernels for 1%

profile of v7, /device:TPU:1, one launch (start us, length us, event | category | flops | bytes accessed | tf_op | source)
XLA Modules:
  0.0 123.8 jit_solution(1560624198505810449)
XLA Ops:
  0.0 8.6 %all_gather.6.x_ref = bf16[128,256]{1,0:T(8,128)(2,1)S(1)} all-gather(bf16[64,256]{1,0:T(8,128)(2,1)} %param.8), channel_id=1, replica_groups=mesh['y'=4,'xh'=2,'c'=2,'z3'=2,'z2'=2,'z1'=2,'z0'=2,'xl'=2] {'c'}, dimensions={0}, use_global_device_ids=true | all-gather | bytes 98304 | tf_op jit(solution)/shard_map/all_gather | solution.py:166
  8.6 0.7 add_bitcast_fusion.code_ref
  9.3 1.3 %dispatch.1 = bf16[256,640]{1,0:T(8,128)(2,1)} custom-call(bf16[128,256]{1,0:T(8,128)(2,1)S(1)} %all_gather.6.x_ref, s32[8,64]{1,0:T(8,128)S(1)} %add_bitcast_fusion.code_ref), custom_call_target="tpu_custom_call" | custom-call | tf_op jit(solution)/shard_map/dispatch/pallas_call | solution.py:18
  10.6 10.8 %all-to-all-start = ((bf16[32,8,640]{2,1,0:T(8,128)(2,1)}), bf16[32,8,640]{2,1,0:T(8,128)(2,1)S(1)}, u32[]{:S(2)}, u32[]{:S(2)}) async-start(bf16[32,8,640]{2,1,0:T(8,128)(2,1)} %bitcast.1), calls=%async_computation | async-start | bytes 655360 | tf_op jit(solution)/shard_map/all_to_all | solution.py:170
  21.4 2.5 %collective-permute-start = (bf16[256,1536]{1,0:T(8,128)(2,1)}, bf16[256,1536]{1,0:T(8,128)(2,1)S(1)}, u32[]{:S(2)}, u32[]{:S(2)}) collective-permute-start(bf16[256,1536]{1,0:T(8,128)(2,1)} %bitcast.21), channel_id=1, source_target_pairs={{0,32},{32,0},{1,33},{33,1},{2,34},{34,2},{3,35},{35,3},{4,36},{36... | collective-permute-start | bytes 2359304 | tf_op jit(solution)/shard_map/ppermute | solution.py:162
  23.9 1.9 %collective-permute-start.1 = (bf16[256,1536]{1,0:T(8,128)(2,1)}, bf16[256,1536]{1,0:T(8,128)(2,1)S(1)}, u32[]{:S(2)}, u32[]{:S(2)}) collective-permute-start(bf16[256,1536]{1,0:T(8,128)(2,1)} %bitcast.23), channel_id=1, source_target_pairs={{0,32},{32,0},{1,33},{33,1},{2,34},{34,2},{3,35},{35,3},{4,36},{36... | collective-permute-start | bytes 2359304 | tf_op jit(solution)/shard_map/ppermute | solution.py:162
  25.8 2.4 %collective-permute-start.2 = (bf16[1536,256]{1,0:T(8,128)(2,1)}, bf16[1536,256]{1,0:T(8,128)(2,1)S(1)}, u32[]{:S(2)}, u32[]{:S(2)}) collective-permute-start(bf16[1536,256]{1,0:T(8,128)(2,1)} %bitcast.25), channel_id=1, source_target_pairs={{0,32},{32,0},{1,33},{33,1},{2,34},{34,2},{3,35},{35,3},{4,36},{36... | collective-permute-start | bytes 2359304 | tf_op jit(solution)/shard_map/ppermute | solution.py:162
  28.3 0.0 copy-start.8
  28.3 0.7 copy-done.8
  29.0 0.6 weigh.1.__.m_ref
  29.5 0.0 collective-permute-done.gb_ref
  29.5 0.0 collective-permute-done.1.ub_ref
  29.5 0.8 collective-permute-done.2._.v_ref
  30.4 0.0 copy-start.4
  30.4 1.1 copy-done.4
  31.5 0.0 copy-start.5
  31.5 1.1 copy-done.5
  32.6 0.2 stack.1.w_ref
  32.8 0.0 copy-start
  32.8 0.9 copy-done
  33.7 0.0 copy-start.2
  33.8 0.7 copy-done.2
  34.4 3.8 %all-to-all-done = bf16[32,8,640]{2,1,0:T(8,128)(2,1)S(1)} async-done(((bf16[32,8,640]{2,1,0:T(8,128)(2,1)}), bf16[32,8,640]{2,1,0:T(8,128)(2,1)S(1)}, u32[]{:S(2)}, u32[]{:S(2)}) %all-to-all-start) | async-done | bytes 327712 | tf_op jit(solution)/shard_map/all_to_all | solution.py:170
  38.2 1.2 gate_up.1
  39.4 28.2 %all_to_all.44 = bf16[8,40,3072]{2,1,0:T(8,128)(2,1)S(1)} all-to-all(bf16[8,40,3072]{2,1,0:T(8,128)(2,1)S(1)} %bitcast.14), channel_id=1, replica_groups=mesh['y'=4,'xh'=2,'c'=2,'z3'=2,'z2'=2,'z1'=2,'z0'=2,'xl'=2] {'y','xh'}, dimensions={0} | all-to-all | bytes 3932160 | tf_op jit(solution)/shard_map/all_to_all | solution.py:170
  67.6 0.0 copy-start.1
  67.6 0.0 copy-start.6
  67.6 0.4 act.1
  68.0 14.5 %all_to_all.45 = bf16[8,40,1536]{2,1,0:T(8,128)(2,1)S(1)} all-to-all(bf16[8,40,1536]{2,1,0:T(8,128)(2,1)S(1)} %bitcast.17), channel_id=1, replica_groups=mesh['y'=4,'xh'=2,'c'=2,'z3'=2,'z2'=2,'z1'=2,'z0'=2,'xl'=2] {'y','xh'}, dimensions={0} | all-to-all | bytes 1966080 | tf_op jit(solution)/shard_map/all_to_all | solution.py:170
  82.5 0.0 copy-start.3
  82.5 0.0 copy-done.1
  82.5 0.0 copy-done.6
  82.5 0.0 copy-start.7
  82.5 0.7 down.1
  83.2 30.5 %all_to_all.46 = bf16[32,8,640]{2,1,0:T(8,128)(2,1)S(1)} all-to-all(bf16[32,8,640]{2,1,0:T(8,128)(2,1)S(1)} %bitcast.20), channel_id=1, replica_groups=mesh['y'=4,'xh'=2,'c'=2,'z3'=2,'z2'=2,'z1'=2,'z0'=2,'xl'=2] {'xl','z0','..., dimensions={0} | all-to-all | bytes 655360 | tf_op jit(solution)/shard_map/all_to_all | solution.py:170
  113.7 0.0 copy-done.3
  113.7 0.3 combine.1
  114.0 9.2 %all_gather.7.sent_ref = f32[128,256]{1,0:T(8,128)S(1)} all-gather(f32[64,256]{1,0:T(8,128)S(1)} %get-tuple-element.8), channel_id=1, replica_groups=mesh['y'=4,'xh'=2,'c'=2,'z3'=2,'z2'=2,'z1'=2,'z0'=2,'xl'=2] {'c'}, dimensions={0}, use_global_device_ids=true | all-gather | bytes 196608 | tf_op jit(solution)/shard_map/all_gather | solution.py:166
  123.2 0.0 copy-done.7
  123.2 0.6 finish.1
Async XLA Ops:
  10.6 27.6 %all-to-all-start = ((bf16[32,8,640]{2,1,0:T(8,128)(2,1)}), bf16[32,8,640]{2,1,0:T(8,128)(2,1)S(1)}, u32[]{:S(2)}, u32[]{:S(2)}) async-start(bf16[32,8,640]{2,1,0:T(8,128)(2,1)} %bitcast.1), calls=%async_computation | async-start | bytes 655360 | tf_op jit(solution)/shard_map/all_to_all | solution.py:170
  21.4 8.1 %collective-permute-start = (bf16[256,1536]{1,0:T(8,128)(2,1)}, bf16[256,1536]{1,0:T(8,128)(2,1)S(1)}, u32[]{:S(2)}, u32[]{:S(2)}) collective-permute-start(bf16[256,1536]{1,0:T(8,128)(2,1)} %bitcast.21), channel_id=1, source_target_pairs={{0,32},{32,0},{1,33},{33,1},{2,34},{34,2},{3,35},{35,3},{4,36},{36... | collective-permute-start | bytes 2359304 | tf_op jit(solution)/shard_map/ppermute | solution.py:162
  23.9 5.6 %collective-permute-start.1 = (bf16[256,1536]{1,0:T(8,128)(2,1)}, bf16[256,1536]{1,0:T(8,128)(2,1)S(1)}, u32[]{:S(2)}, u32[]{:S(2)}) collective-permute-start(bf16[256,1536]{1,0:T(8,128)(2,1)} %bitcast.23), channel_id=1, source_target_pairs={{0,32},{32,0},{1,33},{33,1},{2,34},{34,2},{3,35},{35,3},{4,36},{36... | collective-permute-start | bytes 2359304 | tf_op jit(solution)/shard_map/ppermute | solution.py:162
  25.8 4.5 %collective-permute-start.2 = (bf16[1536,256]{1,0:T(8,128)(2,1)}, bf16[1536,256]{1,0:T(8,128)(2,1)S(1)}, u32[]{:S(2)}, u32[]{:S(2)}) collective-permute-start(bf16[1536,256]{1,0:T(8,128)(2,1)} %bitcast.25), channel_id=1, source_target_pairs={{0,32},{32,0},{1,33},{33,1},{2,34},{34,2},{3,35},{35,3},{4,36},{36... | collective-permute-start | bytes 2359304 | tf_op jit(solution)/shard_map/ppermute | solution.py:162
  28.3 0.7 copy-start.8
  30.4 1.1 copy-start.4
  31.5 1.1 copy-start.5
  32.8 0.9 copy-start
  33.7 0.7 copy-start.2
  67.6 14.9 %copy-start.1 = (bf16[1536,256]{1,0:T(8,128)(2,1)S(1)}, bf16[1536,256]{1,0:T(8,128)(2,1)}, u32[]{:S(2)}) copy-start(bf16[1536,256]{1,0:T(8,128)(2,1)} %copy-done) | copy-start | bytes 2359300
  67.6 14.9 %copy-start.6 = (bf16[1,1536,256]{2,1,0:T(8,128)(2,1)S(1)}, bf16[1,1536,256]{2,1,0:T(8,128)(2,1)}, u32[]{:S(2)}) copy-start(bf16[1,1536,256]{2,1,0:T(8,128)(2,1)} %param.12) | copy-start | bytes 2359300
  82.5 31.2 %copy-start.3 = (bf16[256,256]{1,0:T(8,128)(2,1)S(1)}, bf16[256,256]{1,0:T(8,128)(2,1)}, u32[]{:S(2)}) copy-start(bf16[256,256]{1,0:T(8,128)(2,1)} %copy-done.2) | copy-start | bytes 393220
  82.5 40.7 %copy-start.7 = (bf16[64,256]{1,0:T(8,128)(2,1)S(1)}, bf16[64,256]{1,0:T(8,128)(2,1)}, u32[]{:S(2)}) copy-start(bf16[64,256]{1,0:T(8,128)(2,1)} %res_ref.1) | copy-start | bytes 98308

commit v8 on v7

--- a/solution.py
+++ b/solution.py
@@ -10,7 +10,7 @@
 T = ("y", "xh", "c")
 R = ("y", "xh")
 E = ("z3", "z2", "z1", "z0", "xl")
-LINE = ("xl", "z0", "z1", "z3", "z2")
+LINE = ("xl", "z2", "z1", "z0", "z3")
 VMEM = pl.BlockSpec(memory_space=pltpu.VMEM)
 
 

time: 124 us -> 129 us (1.040)
  waiting for transfers between devices: 4.59 us -> 9.61 us
    all_to_all x1, waiting for transfers between devices: 3.76 us -> 8.77 us  [spread(): return lax.all_to_all(x, axes, split_axis=0, concat_axis=0, tiled=True)]
    all_gather x2, blocking collectives: 17.8 us -> 15.8 us  [share(): return lax.all_gather(x, 'c', axis=0, tiled=True)]
    all_to_all x3, blocking collectives: 73.2 us -> 74.6 us  [spread(): return lax.all_to_all(x, axes, split_axis=0, concat_axis=0, tiled=True)]
where the time goes in v8:
time: 129 us; the launch traced here: 128 us
  blocking collectives  90.4 us (70%)
  starting transfers between devices  17.6 us (14%)
  waiting for transfers between devices  9.61 us (7%)
  Pallas kernels  5.25 us (4%)
  local copies, waits for them, and re-layouts  4.53 us (4%)
    all_to_all x3, blocking collectives, spread(): return lax.all_to_all(x, axes, split_axis=0, concat_axis=0, tiled=True)  74.6 us
    all_gather x2, blocking collectives, share(): return lax.all_gather(x, 'c', axis=0, tiled=True)  15.8 us
    all_to_all x1, starting transfers between devices, spread(): return lax.all_to_all(x, axes, split_axis=0, concat_axis=0, tiled=True)  10.8 us
    all_to_all x1, waiting for transfers between devices, spread(): return lax.all_to_all(x, axes, split_axis=0, concat_axis=0, tiled=True)  8.77 us
    ppermute x3, starting transfers between devices, swap(): return lax.ppermute(x, 'c', [(0, 1), (1, 0)])  6.87 us
    pallas_call x8, Pallas kernels, call(): pl.pallas_call(body, out_shape=out, in_specs=[VMEM] * len(args), out_spec...  5.25 us
    unnamed x18, local copies, waits for them, and re-layouts  4.53 us
  transfers between devices with their start and end apart: 4, of which 2 were waited for; matrix products, arithmetic and copies ran while one was open for 0% of the time, Pallas kernels for 1%

profile of v8, /device:TPU:1, one launch (start us, length us, event | category | flops | bytes accessed | tf_op | source)
XLA Modules:
  0.0 128.3 jit_solution(15332704595913292153)
XLA Ops:
  0.0 8.6 %all_gather.6.x_ref = bf16[128,256]{1,0:T(8,128)(2,1)S(1)} all-gather(bf16[64,256]{1,0:T(8,128)(2,1)} %param.8), channel_id=1, replica_groups=mesh['y'=4,'xh'=2,'c'=2,'z3'=2,'z2'=2,'z1'=2,'z0'=2,'xl'=2] {'c'}, dimensions={0}, use_global_device_ids=true | all-gather | bytes 98304 | tf_op jit(solution)/shard_map/all_gather | solution.py:166
  8.6 0.7 add_bitcast_fusion.code_ref
  9.3 1.3 %dispatch.1 = bf16[256,640]{1,0:T(8,128)(2,1)} custom-call(bf16[128,256]{1,0:T(8,128)(2,1)S(1)} %all_gather.6.x_ref, s32[8,64]{1,0:T(8,128)S(1)} %add_bitcast_fusion.code_ref), custom_call_target="tpu_custom_call" | custom-call | tf_op jit(solution)/shard_map/dispatch/pallas_call | solution.py:18
  10.6 10.8 %all-to-all-start = ((bf16[32,8,640]{2,1,0:T(8,128)(2,1)}), bf16[32,8,640]{2,1,0:T(8,128)(2,1)S(1)}, u32[]{:S(2)}, u32[]{:S(2)}) async-start(bf16[32,8,640]{2,1,0:T(8,128)(2,1)} %bitcast.1), calls=%async_computation | async-start | bytes 655360 | tf_op jit(solution)/shard_map/all_to_all | solution.py:170
  21.4 2.5 %collective-permute-start = (bf16[256,1536]{1,0:T(8,128)(2,1)}, bf16[256,1536]{1,0:T(8,128)(2,1)S(1)}, u32[]{:S(2)}, u32[]{:S(2)}) collective-permute-start(bf16[256,1536]{1,0:T(8,128)(2,1)} %bitcast.21), channel_id=1, source_target_pairs={{0,32},{32,0},{1,33},{33,1},{2,34},{34,2},{3,35},{35,3},{4,36},{36... | collective-permute-start | bytes 2359304 | tf_op jit(solution)/shard_map/ppermute | solution.py:162
  23.9 1.9 %collective-permute-start.1 = (bf16[256,1536]{1,0:T(8,128)(2,1)}, bf16[256,1536]{1,0:T(8,128)(2,1)S(1)}, u32[]{:S(2)}, u32[]{:S(2)}) collective-permute-start(bf16[256,1536]{1,0:T(8,128)(2,1)} %bitcast.23), channel_id=1, source_target_pairs={{0,32},{32,0},{1,33},{33,1},{2,34},{34,2},{3,35},{35,3},{4,36},{36... | collective-permute-start | bytes 2359304 | tf_op jit(solution)/shard_map/ppermute | solution.py:162
  25.8 2.4 %collective-permute-start.2 = (bf16[1536,256]{1,0:T(8,128)(2,1)}, bf16[1536,256]{1,0:T(8,128)(2,1)S(1)}, u32[]{:S(2)}, u32[]{:S(2)}) collective-permute-start(bf16[1536,256]{1,0:T(8,128)(2,1)} %bitcast.25), channel_id=1, source_target_pairs={{0,32},{32,0},{1,33},{33,1},{2,34},{34,2},{3,35},{35,3},{4,36},{36... | collective-permute-start | bytes 2359304 | tf_op jit(solution)/shard_map/ppermute | solution.py:162
  28.3 0.0 copy-start.8
  28.3 0.7 copy-done.8
  29.0 0.6 weigh.1.__.m_ref
  29.5 0.0 collective-permute-done.gb_ref
  29.5 0.0 collective-permute-done.1.ub_ref
  29.5 0.8 collective-permute-done.2._.v_ref
  30.4 0.0 copy-start.4
  30.4 1.1 copy-done.4
  31.5 0.0 copy-start.5
  31.5 1.1 copy-done.5
  32.6 0.2 stack.1.w_ref
  32.8 0.0 copy-start
  32.8 0.9 copy-done
  33.7 0.0 copy-start.2
  33.8 0.7 copy-done.2
  34.4 8.8 %all-to-all-done = bf16[32,8,640]{2,1,0:T(8,128)(2,1)S(1)} async-done(((bf16[32,8,640]{2,1,0:T(8,128)(2,1)}), bf16[32,8,640]{2,1,0:T(8,128)(2,1)S(1)}, u32[]{:S(2)}, u32[]{:S(2)}) %all-to-all-start) | async-done | bytes 327712 | tf_op jit(solution)/shard_map/all_to_all | solution.py:170
  43.2 1.2 gate_up.1
  44.4 29.6 %all_to_all.44 = bf16[8,40,3072]{2,1,0:T(8,128)(2,1)S(1)} all-to-all(bf16[8,40,3072]{2,1,0:T(8,128)(2,1)S(1)} %bitcast.14), channel_id=1, replica_groups=mesh['y'=4,'xh'=2,'c'=2,'z3'=2,'z2'=2,'z1'=2,'z0'=2,'xl'=2] {'y','xh'}, dimensions={0} | all-to-all | bytes 3932160 | tf_op jit(solution)/shard_map/all_to_all | solution.py:170
  74.0 0.0 copy-start.1
  74.0 0.0 copy-start.6
  74.0 0.4 act.1
  74.5 14.7 %all_to_all.45 = bf16[8,40,1536]{2,1,0:T(8,128)(2,1)S(1)} all-to-all(bf16[8,40,1536]{2,1,0:T(8,128)(2,1)S(1)} %bitcast.17), channel_id=1, replica_groups=mesh['y'=4,'xh'=2,'c'=2,'z3'=2,'z2'=2,'z1'=2,'z0'=2,'xl'=2] {'y','xh'}, dimensions={0} | all-to-all | bytes 1966080 | tf_op jit(solution)/shard_map/all_to_all | solution.py:170
  89.2 0.0 copy-start.3
  89.2 0.0 copy-done.1
  89.2 0.0 copy-done.6
  89.2 0.0 copy-start.7
  89.2 0.7 down.1
  89.9 30.3 %all_to_all.46 = bf16[32,8,640]{2,1,0:T(8,128)(2,1)S(1)} all-to-all(bf16[32,8,640]{2,1,0:T(8,128)(2,1)S(1)} %bitcast.20), channel_id=1, replica_groups=mesh['y'=4,'xh'=2,'c'=2,'z3'=2,'z2'=2,'z1'=2,'z0'=2,'xl'=2] {'xl','z2','..., dimensions={0} | all-to-all | bytes 655360 | tf_op jit(solution)/shard_map/all_to_all | solution.py:170
  120.1 0.0 copy-done.3
  120.1 0.3 combine.1
  120.4 7.2 %all_gather.7.sent_ref = f32[128,256]{1,0:T(8,128)S(1)} all-gather(f32[64,256]{1,0:T(8,128)S(1)} %get-tuple-element.8), channel_id=1, replica_groups=mesh['y'=4,'xh'=2,'c'=2,'z3'=2,'z2'=2,'z1'=2,'z0'=2,'xl'=2] {'c'}, dimensions={0}, use_global_device_ids=true | all-gather | bytes 196608 | tf_op jit(solution)/shard_map/all_gather | solution.py:166
  127.6 0.0 copy-done.7
  127.6 0.6 finish.1
Async XLA Ops:
  10.6 32.6 %all-to-all-start = ((bf16[32,8,640]{2,1,0:T(8,128)(2,1)}), bf16[32,8,640]{2,1,0:T(8,128)(2,1)S(1)}, u32[]{:S(2)}, u32[]{:S(2)}) async-start(bf16[32,8,640]{2,1,0:T(8,128)(2,1)} %bitcast.1), calls=%async_computation | async-start | bytes 655360 | tf_op jit(solution)/shard_map/all_to_all | solution.py:170
  21.4 8.1 %collective-permute-start = (bf16[256,1536]{1,0:T(8,128)(2,1)}, bf16[256,1536]{1,0:T(8,128)(2,1)S(1)}, u32[]{:S(2)}, u32[]{:S(2)}) collective-permute-start(bf16[256,1536]{1,0:T(8,128)(2,1)} %bitcast.21), channel_id=1, source_target_pairs={{0,32},{32,0},{1,33},{33,1},{2,34},{34,2},{3,35},{35,3},{4,36},{36... | collective-permute-start | bytes 2359304 | tf_op jit(solution)/shard_map/ppermute | solution.py:162
  23.9 5.6 %collective-permute-start.1 = (bf16[256,1536]{1,0:T(8,128)(2,1)}, bf16[256,1536]{1,0:T(8,128)(2,1)S(1)}, u32[]{:S(2)}, u32[]{:S(2)}) collective-permute-start(bf16[256,1536]{1,0:T(8,128)(2,1)} %bitcast.23), channel_id=1, source_target_pairs={{0,32},{32,0},{1,33},{33,1},{2,34},{34,2},{3,35},{35,3},{4,36},{36... | collective-permute-start | bytes 2359304 | tf_op jit(solution)/shard_map/ppermute | solution.py:162
  25.8 4.5 %collective-permute-start.2 = (bf16[1536,256]{1,0:T(8,128)(2,1)}, bf16[1536,256]{1,0:T(8,128)(2,1)S(1)}, u32[]{:S(2)}, u32[]{:S(2)}) collective-permute-start(bf16[1536,256]{1,0:T(8,128)(2,1)} %bitcast.25), channel_id=1, source_target_pairs={{0,32},{32,0},{1,33},{33,1},{2,34},{34,2},{3,35},{35,3},{4,36},{36... | collective-permute-start | bytes 2359304 | tf_op jit(solution)/shard_map/ppermute | solution.py:162
  28.3 0.7 copy-start.8
  30.4 1.1 copy-start.4
  31.5 1.1 copy-start.5
  32.8 0.9 copy-start
  33.7 0.7 copy-start.2
  74.0 15.1 %copy-start.1 = (bf16[1536,256]{1,0:T(8,128)(2,1)S(1)}, bf16[1536,256]{1,0:T(8,128)(2,1)}, u32[]{:S(2)}) copy-start(bf16[1536,256]{1,0:T(8,128)(2,1)} %copy-done) | copy-start | bytes 2359300
  74.0 15.1 %copy-start.6 = (bf16[1,1536,256]{2,1,0:T(8,128)(2,1)S(1)}, bf16[1,1536,256]{2,1,0:T(8,128)(2,1)}, u32[]{:S(2)}) copy-start(bf16[1,1536,256]{2,1,0:T(8,128)(2,1)} %param.12) | copy-start | bytes 2359300
  89.2 31.0 %copy-start.3 = (bf16[256,256]{1,0:T(8,128)(2,1)S(1)}, bf16[256,256]{1,0:T(8,128)(2,1)}, u32[]{:S(2)}) copy-start(bf16[256,256]{1,0:T(8,128)(2,1)} %copy-done.2) | copy-start | bytes 393220
  89.2 38.5 %copy-start.7 = (bf16[64,256]{1,0:T(8,128)(2,1)S(1)}, bf16[64,256]{1,0:T(8,128)(2,1)}, u32[]{:S(2)}) copy-start(bf16[64,256]{1,0:T(8,128)(2,1)} %res_ref.1) | copy-start | bytes 98308
